TPU v7x, 256 devices: a whole 4x4x8 slice. The times are simulated.
256 devices in a mesh: sy: 8 (over x_hi, y), sx: 2 (over core), grp: 16 (over z, x_lo).
Axes of the slice: x: 4 (x_hi: 2, x_lo: 2; x = x_hi * 2 + x_lo), y: 4, z: 8, core: 2. Of those that a mesh axis runs over, the one named last changes fastest.
Arguments:
- image: bfloat16 [16, 64, 256, 256], P('grp', None, 'sy', 'sx'), may hold values from -6 to 6
- weight_one: bfloat16 [3, 3, 64, 64], replicated, may hold values from -0.25 to 0.25
- bias_one: float32 [64], replicated, may hold values from -3 to 3
- weight_two: bfloat16 [3, 3, 64, 64], replicated, may hold values from -0.25 to 0.25
- bias_two: float32 [64], replicated, may hold values from -3 to 3
- cotangent: bfloat16 [16, 64, 256, 256], P('grp', None, 'sy', 'sx'), may hold values from -51 to 51
Outputs:
- output: bfloat16 [16, 64, 256, 256], P('grp', None, 'sy', 'sx')
- image_grad: bfloat16 [16, 64, 256, 256], P('grp', None, 'sy', 'sx')
- grad_weight_one: float32 [3, 3, 64, 64], replicated
- grad_bias_one: float32 [64], replicated
- grad_weight_two: float32 [3, 3, 64, 64], replicated
- grad_bias_two: float32 [64], replicated
All inputs are finite; a program needn't handle non-finite values.
Results may differ from a plain program's by a relative error of at most 0.0075.
Values may be sent and summed in bfloat16 or wider, within the bound.
A program may use at most 64 MiB of HBM per device.

v0:
```python
import jax
import jax.numpy as jnp
from jax import lax
from jax.sharding import PartitionSpec as P


def extended(block, sides, width):
    for axis, dim in sides:
        count = lax.axis_size(axis)
        forward = [(i, i + 1) for i in range(count - 1)]
        backward = [(target, source) for source, target in forward]
        low = lax.ppermute(
            lax.slice_in_dim(block, block.shape[dim] - width, None, axis=dim), axis, forward
        )
        high = lax.ppermute(lax.slice_in_dim(block, 0, width, axis=dim), axis, backward)
        block = jnp.concatenate([low, block, high], axis=dim)
    return block


def convolve(padded, kernel):
    return lax.conv_general_dilated(
        padded,
        kernel,
        (1, 1),
        "VALID",
        dimension_numbers=("NCHW", "HWIO", "NCHW"),
        preferred_element_type=jnp.float32,
    )


def flipped(kernel):
    return jnp.transpose(kernel[::-1, ::-1], (0, 1, 3, 2))


def kernel_grad(padded, delta):
    rows = delta.shape[2]
    cols = delta.shape[3]
    taps = []
    for row_tap in range(3):
        for col_tap in range(3):
            window = padded[0, :, row_tap : row_tap + rows, col_tap : col_tap + cols]
            taps.append(
                jnp.einsum("ihw,ohw->io", window, delta[0], preferred_element_type=jnp.float32)
            )
    return jnp.stack(taps).reshape(3, 3, delta.shape[1], delta.shape[1])


def slope(pre):
    gate = jax.nn.sigmoid(pre)
    return gate * (1.0 + pre * (1.0 - gate))


def local(image, weight_one, bias_one, weight_two, bias_two, cotangent):
    rows = image.shape[2]
    cols = image.shape[3]
    shift_one = bias_one.reshape(1, -1, 1, 1)
    shift_two = bias_two.reshape(1, -1, 1, 1)
    image_pad = extended(image, (("sy", 2), ("sx", 3)), 1)
    pre_one = convolve(image_pad, weight_one) + shift_one
    hidden = (pre_one * jax.nn.sigmoid(pre_one)).astype(jnp.bfloat16)
    hidden_pad = extended(hidden, (("sy", 2), ("sx", 3)), 1)
    pre_two = convolve(hidden_pad, weight_two) + shift_two
    output = (pre_two * jax.nn.sigmoid(pre_two)).astype(jnp.bfloat16)
    delta_two = (cotangent.astype(jnp.float32) * slope(pre_two)).astype(jnp.bfloat16)
    grad_two = kernel_grad(hidden_pad, delta_two)
    bias_grad_two = jnp.sum(delta_two, axis=(0, 2, 3), dtype=jnp.float32)
    factor = (rows * cols * lax.axis_size("sy") * lax.axis_size("sx") * lax.axis_size("grp")) ** (
        -0.5
    )
    delta_pad = extended(delta_two, (("sy", 2), ("sx", 3)), 1)
    hidden_grad = convolve(delta_pad, flipped(weight_two))
    delta_one = (hidden_grad * slope(pre_one)).astype(jnp.bfloat16)
    grad_one = kernel_grad(image_pad, delta_one)
    bias_grad_one = jnp.sum(delta_one, axis=(0, 2, 3), dtype=jnp.float32)
    inner_pad = extended(delta_one, (("sy", 2), ("sx", 3)), 1)
    image_grad = convolve(inner_pad, flipped(weight_one)).astype(jnp.bfloat16)
    summed_one, summed_bias_one, summed_two, summed_bias_two = lax.psum(
        (grad_one, bias_grad_one, grad_two, bias_grad_two), ("sy", "sx", "grp")
    )
    return (
        output,
        image_grad,
        summed_one * factor,
        summed_bias_one * factor,
        summed_two * factor,
        summed_bias_two * factor,
    )


def solution(mesh):
    return jax.shard_map(
        local,
        mesh=mesh,
        in_specs=(P("grp", None, "sy", "sx"), P(), P(), P(), P(), P("grp", None, "sy", "sx")),
        out_specs=(P("grp", None, "sy", "sx"), P("grp", None, "sy", "sx"), P(), P(), P(), P()),
        check_vma=False,
    )
```

profile of v0, /device:TPU:1, one launch (start us, length us, event | category | flops | bytes accessed | tf_op | source)
XLA Modules:
  0.0 387.8 jit_solution(8790171705123593679)
XLA Ops:
  8.5 4.0 %collective-permute-start = (bf16[1,64,1,128]{3,1,2,0:T(8,128)(2,1)S(1)}, bf16[1,64,1,128]{3,1,2,0:T(8,128)(2,1)S(1)}, u32[]{:S(2)}, u32[]{:S(2)}) collective-permute-start(bf16[1,64,1,128]{3,1,2,0:T(8,128)(2,1)S(1)} %get-tuple-element.55), channel_id=1, source_target_pairs={{0,32},{32,64},{64,96},{96,128},{128,160},{160,192},{192,224},{1,3... | collective-permute-start | bytes 49160 | tf_op jit(solution)/shard_map/ppermute | solution.py:12
  12.6 1.3 collective-permute-start.1
  15.2 1.9 collective-permute-done.1
  18.2 4.0 %collective-permute-start.3 = (bf16[1,64,34,1]{1,2,3,0:T(8,128)(2,1)S(1)}, bf16[1,64,34,1]{1,2,3,0:T(8,128)(2,1)S(1)}, u32[]{:S(2)}, u32[]{:S(2)}) collective-permute-start(bf16[1,64,34,1]{1,2,3,0:T(8,128)(2,1)S(1)} %copy.211), channel_id=1, source_target_pairs={{16,0},{17,1},{18,2},{19,3},{20,4},{21,5},{22,6},{23,7},{24,8},{25... | collective-permute-start | bytes 13064 | tf_op jit(solution)/shard_map/ppermute | solution.py:15
  24.3 1.4 collective-permute-done.2
  26.8 1.7 maximum_bitcast_fusion.1
  28.5 3.0 copy.276
  32.7 3.2 multiply_convert_fusion.2
  37.6 4.0 %collective-permute-start.4 = (bf16[1,64,1,128]{3,1,2,0:T(8,128)(2,1)S(1)}, bf16[1,64,1,128]{3,1,2,0:T(8,128)(2,1)S(1)}, u32[]{:S(2)}, u32[]{:S(2)}) collective-permute-start(bf16[1,64,1,128]{3,1,2,0:T(8,128)(2,1)S(1)} %bitcast.256), channel_id=1, source_target_pairs={{0,32},{32,64},{64,96},{96,128},{128,160},{160,192},{192,224},{1,3... | collective-permute-start | bytes 49160 | tf_op jit(solution)/shard_map/ppermute | solution.py:12
  43.7 2.6 collective-permute-start.7
  46.6 1.7 collective-permute-start.6
  48.4 2.6 copy.231
  53.0 1.6 maximum_bitcast_fusion.2
  54.6 3.0 copy.277
  58.6 2.2 add_multiply_fusion
  66.4 4.5 %collective-permute-start.8 = (bf16[1,64,1,128]{1,2,3,0:T(2,128)(2,1)}, bf16[1,64,1,128]{1,2,3,0:T(2,128)(2,1)S(1)}, u32[]{:S(2)}, u32[]{:S(2)}) collective-permute-start(bf16[1,64,1,128]{1,2,3,0:T(2,128)(2,1)} %get-tuple-element.44), channel_id=1, source_target_pairs={{0,32},{32,64},{64,96},{96,128},{128,160},{160,192},{192,224},{1,3... | collective-permute-start | bytes 49160 | tf_op jit(solution)/shard_map/ppermute | solution.py:12
  71.0 1.9 copy.256
  72.9 1.8 pad_maximum_fusion
  82.1 3.3 collective-permute-start.11
  85.4 1.5 collective-permute-start.10
  87.8 3.6 copy.266
  94.1 3.5 select_reduce_fusion
  98.0 1.4 collective-permute-start.13
  100.5 2.3 copy.274
  102.9 7.1 %collective-permute-start.12 = (bf16[1,64,1,128]{3,1,2,0:T(8,128)(2,1)S(1)}, bf16[1,64,1,128]{3,1,2,0:T(8,128)(2,1)S(1)}, u32[]{:S(2)}, u32[]{:S(2)}) collective-permute-start(bf16[1,64,1,128]{3,1,2,0:T(8,128)(2,1)S(1)} %bitcast.254), channel_id=1, source_target_pairs={{0,32},{32,64},{64,96},{96,128},{128,160},{160,192},{192,224},{1,3... | collective-permute-start | bytes 49160 | tf_op jit(solution)/shard_map/ppermute | solution.py:12
  114.5 92.1 %all-reduce = (f32[64]{0:T(128)S(1)}, f32[64]{0:T(128)S(1)}) all-reduce(f32[64]{0:T(128)S(1)} %get-tuple-element.58, f32[64]{0:T(128)S(1)} %copy-done.17), channel_id=1, replica_groups=mesh['sy'=8,'sx'=2,'grp'=16] {'sy','sx','grp'}, use_global_device_ids=true, to_apply=%region_2.0 | all-reduce | flops 128 | bytes 1024 | tf_op jit(solution)/shard_map/psum | solution.py:77
  207.3 3.1 collective-permute-start.15
  214.8 1.9 copy.278
  217.9 2.8 select_convert_fusion
  221.0 2.3 copy.267
  223.3 155.6 %all-reduce.4.cloned.1.call-done = (f32[3,3,64,64]{3,2,1,0:T(8,128)}, f32[3,3,64,64]{3,2,1,0:T(8,128)}) async-done(((f32[3,3,64,64]{3,2,1,0:T(8,128)}, f32[3,3,64,64]{3,2,1,0:T(8,128)}), (f32[3,3,64,64]{3,2,1,0:T(8,128)}, f32[3,3,64,64]{3,2,1,0:T(8,128)})) %all-reduce.4.cloned.1.call-update) | async-done | bytes 294928 | tf_op jit(solution)/shard_map/psum | solution.py:77
  378.9 1.9 broadcast_multiply_fusion
  (158 shorter events, 43.8 us)
Async XLA Ops:
  7.2 51.0 %copy-start = (bf16[3,3,64,64]{3,2,1,0:T(8,128)(2,1)S(1)}, bf16[3,3,64,64]{3,2,1,0:T(8,128)(2,1)}, u32[]{:S(2)}) copy-start(bf16[3,3,64,64]{3,2,1,0:T(8,128)(2,1)} %param.9) | copy-start | bytes 221188
  7.2 371.7 %all-reduce.4.cloned.1.call-start = ((), (), s32[]{:S(2)}) async-start(), calls=%async_computation | async-start | bytes 1179648 | tf_op jit(solution)/shard_map/psum | solution.py:77
  8.5 5.4 %copy-start.9 = (bf16[1,64,32,128]{3,1,2,0:T(8,128)(2,1)}, bf16[1,64,32,128]{3,1,2,0:T(8,128)(2,1)S(1)}, u32[]{:S(2)}) copy-start(bf16[1,64,32,128]{3,1,2,0:T(8,128)(2,1)S(1)} %copy.207) | copy-start | bytes 1572868
  8.5 5.4 %collective-permute-start = (bf16[1,64,1,128]{3,1,2,0:T(8,128)(2,1)S(1)}, bf16[1,64,1,128]{3,1,2,0:T(8,128)(2,1)S(1)}, u32[]{:S(2)}, u32[]{:S(2)}) collective-permute-start(bf16[1,64,1,128]{3,1,2,0:T(8,128)(2,1)S(1)} %get-tuple-element.55), channel_id=1, source_target_pairs={{0,32},{32,64},{64,96},{96,128},{128,160},{160,192},{192,224},{1,3... | collective-permute-start | bytes 49160 | tf_op jit(solution)/shard_map/ppermute | solution.py:12
  12.6 4.5 %collective-permute-start.1 = (bf16[1,64,1,128]{3,1,2,0:T(8,128)(2,1)S(1)}, bf16[1,64,1,128]{3,1,2,0:T(8,128)(2,1)S(1)}, u32[]{:S(2)}, u32[]{:S(2)}) collective-permute-start(bf16[1,64,1,128]{3,1,2,0:T(8,128)(2,1)S(1)} %get-tuple-element.54), channel_id=1, source_target_pairs={{32,0},{64,32},{96,64},{128,96},{160,128},{192,160},{224,192},{33,... | collective-permute-start | bytes 49160 | tf_op jit(solution)/shard_map/ppermute | solution.py:15
  13.9 3.2 copy-start.15
  18.2 5.6 %collective-permute-start.3 = (bf16[1,64,34,1]{1,2,3,0:T(8,128)(2,1)S(1)}, bf16[1,64,34,1]{1,2,3,0:T(8,128)(2,1)S(1)}, u32[]{:S(2)}, u32[]{:S(2)}) collective-permute-start(bf16[1,64,34,1]{1,2,3,0:T(8,128)(2,1)S(1)} %copy.211), channel_id=1, source_target_pairs={{16,0},{17,1},{18,2},{19,3},{20,4},{21,5},{22,6},{23,7},{24,8},{25... | collective-permute-start | bytes 13064 | tf_op jit(solution)/shard_map/ppermute | solution.py:15
  22.6 3.1 collective-permute-start.2
  36.1 6.8 %collective-permute-start.5 = (bf16[1,64,1,128]{3,1,2,0:T(8,128)(2,1)S(1)}, bf16[1,64,1,128]{3,1,2,0:T(8,128)(2,1)S(1)}, u32[]{:S(2)}, u32[]{:S(2)}) collective-permute-start(bf16[1,64,1,128]{3,1,2,0:T(8,128)(2,1)S(1)} %bitcast.255), channel_id=1, source_target_pairs={{32,0},{64,32},{96,64},{128,96},{160,128},{192,160},{224,192},{33,... | collective-permute-start | bytes 49160 | tf_op jit(solution)/shard_map/ppermute | solution.py:15
  37.6 5.4 %collective-permute-start.4 = (bf16[1,64,1,128]{3,1,2,0:T(8,128)(2,1)S(1)}, bf16[1,64,1,128]{3,1,2,0:T(8,128)(2,1)S(1)}, u32[]{:S(2)}, u32[]{:S(2)}) collective-permute-start(bf16[1,64,1,128]{3,1,2,0:T(8,128)(2,1)S(1)} %bitcast.256), channel_id=1, source_target_pairs={{0,32},{32,64},{64,96},{96,128},{128,160},{160,192},{192,224},{1,3... | collective-permute-start | bytes 49160 | tf_op jit(solution)/shard_map/ppermute | solution.py:12
  43.0 5.4 %copy-start.11 = (bf16[1,64,32,128]{3,2,1,0:T(8,128)(2,1)S(1)}, bf16[1,64,32,128]{3,2,1,0:T(8,128)(2,1)}, u32[]{:S(2)}) copy-start(bf16[1,64,32,128]{3,2,1,0:T(8,128)(2,1)} %param.11) | copy-start | bytes 1572868
  43.7 7.3 %collective-permute-start.7 = (bf16[1,64,34,1]{1,2,3,0:T(8,128)(2,1)S(1)}, bf16[1,64,34,1]{1,2,3,0:T(8,128)(2,1)S(1)}, u32[]{:S(2)}, u32[]{:S(2)}) collective-permute-start(bf16[1,64,34,1]{1,2,3,0:T(8,128)(2,1)S(1)} %copy.224), channel_id=1, source_target_pairs={{16,0},{17,1},{18,2},{19,3},{20,4},{21,5},{22,6},{23,7},{24,8},{25... | collective-permute-start | bytes 13064 | tf_op jit(solution)/shard_map/ppermute | solution.py:15
  46.6 4.7 %collective-permute-start.6 = (bf16[1,64,34,1]{1,2,3,0:T(8,128)(2,1)S(1)}, bf16[1,64,34,1]{1,2,3,0:T(8,128)(2,1)S(1)}, u32[]{:S(2)}, u32[]{:S(2)}) collective-permute-start(bf16[1,64,34,1]{1,2,3,0:T(8,128)(2,1)S(1)} %copy.223), channel_id=1, source_target_pairs={{0,16},{1,17},{2,18},{3,19},{4,20},{5,21},{6,22},{7,23},{8,24},{9,... | collective-permute-start | bytes 13064 | tf_op jit(solution)/shard_map/ppermute | solution.py:12
  62.1 1.2 copy-start.6
  63.3 9.6 %copy-start.4 = (bf16[1,64,34,1]{3,1,2,0:T(8,128)(2,1)S(1)}, bf16[1,64,34,1]{3,1,2,0:T(8,128)(2,1)}, u32[]{:S(2)}) copy-start(bf16[1,64,34,1]{3,1,2,0:T(8,128)(2,1)} %copy-done.3) | copy-start | bytes 13060
  65.1 16.9 %collective-permute-start.9 = (bf16[1,64,1,128]{1,2,3,0:T(2,128)(2,1)}, bf16[1,64,1,128]{1,2,3,0:T(2,128)(2,1)S(1)}, u32[]{:S(2)}, u32[]{:S(2)}) collective-permute-start(bf16[1,64,1,128]{1,2,3,0:T(2,128)(2,1)} %get-tuple-element.45), channel_id=1, source_target_pairs={{32,0},{64,32},{96,64},{128,96},{160,128},{192,160},{224,192},{33,... | collective-permute-start | bytes 49160 | tf_op jit(solution)/shard_map/ppermute | solution.py:15
  66.4 15.6 %collective-permute-start.8 = (bf16[1,64,1,128]{1,2,3,0:T(2,128)(2,1)}, bf16[1,64,1,128]{1,2,3,0:T(2,128)(2,1)S(1)}, u32[]{:S(2)}, u32[]{:S(2)}) collective-permute-start(bf16[1,64,1,128]{1,2,3,0:T(2,128)(2,1)} %get-tuple-element.44), channel_id=1, source_target_pairs={{0,32},{32,64},{64,96},{96,128},{128,160},{160,192},{192,224},{1,3... | collective-permute-start | bytes 49160 | tf_op jit(solution)/shard_map/ppermute | solution.py:12
  72.9 1.8 copy-start.7
  82.1 9.4 %collective-permute-start.11 = (bf16[1,64,34,1]{1,2,3,0:T(8,128)(2,1)S(1)}, bf16[1,64,34,1]{1,2,3,0:T(8,128)(2,1)S(1)}, u32[]{:S(2)}, u32[]{:S(2)}) collective-permute-start(bf16[1,64,34,1]{1,2,3,0:T(8,128)(2,1)S(1)} %get-tuple-element.39), channel_id=1, source_target_pairs={{16,0},{17,1},{18,2},{19,3},{20,4},{21,5},{22,6},{23,7},{24,8},{25... | collective-permute-start | bytes 13064 | tf_op jit(solution)/shard_map/ppermute | solution.py:15
  85.4 6.0 %collective-permute-start.10 = (bf16[1,64,34,1]{1,2,3,0:T(8,128)(2,1)S(1)}, bf16[1,64,34,1]{1,2,3,0:T(8,128)(2,1)S(1)}, u32[]{:S(2)}, u32[]{:S(2)}) collective-permute-start(bf16[1,64,34,1]{1,2,3,0:T(8,128)(2,1)S(1)} %get-tuple-element.38), channel_id=1, source_target_pairs={{0,16},{1,17},{2,18},{3,19},{4,20},{5,21},{6,22},{7,23},{8,24},{9,... | collective-permute-start | bytes 13064 | tf_op jit(solution)/shard_map/ppermute | solution.py:12
  92.4 1.6 copy-start.25
  97.8 12.2 %copy-start.2 = (bf16[1,64,34,1]{3,1,2,0:T(8,128)(2,1)S(1)}, bf16[1,64,34,1]{3,1,2,0:T(8,128)(2,1)}, u32[]{:S(2)}) copy-start(bf16[1,64,34,1]{3,1,2,0:T(8,128)(2,1)} %copy-done.1) | copy-start | bytes 13060
  98.0 108.6 %collective-permute-start.13 = (bf16[1,64,1,128]{3,1,2,0:T(8,128)(2,1)S(1)}, bf16[1,64,1,128]{3,1,2,0:T(8,128)(2,1)S(1)}, u32[]{:S(2)}, u32[]{:S(2)}) collective-permute-start(bf16[1,64,1,128]{3,1,2,0:T(8,128)(2,1)S(1)} %bitcast.253), channel_id=1, source_target_pairs={{32,0},{64,32},{96,64},{128,96},{160,128},{192,160},{224,192},{33,... | collective-permute-start | bytes 49160 | tf_op jit(solution)/shard_map/ppermute | solution.py:15
  100.5 10.0 %copy-start.10 = (bf16[1,64,32,128]{3,1,2,0:T(8,128)(2,1)S(1)}, bf16[1,64,32,128]{3,1,2,0:T(8,128)(2,1)}, u32[]{:S(2)}) copy-start(bf16[1,64,32,128]{3,1,2,0:T(8,128)(2,1)} %copy-done.9) | copy-start | bytes 1572868
  100.5 10.0 %copy-start.16 = (bf16[1,64,1,128]{3,1,2,0:T(8,128)(2,1)S(1)}, bf16[1,64,1,128]{3,1,2,0:T(8,128)(2,1)}, u32[]{:S(2)}) copy-start(bf16[1,64,1,128]{3,1,2,0:T(8,128)(2,1)} %copy-done.15) | copy-start | bytes 49156
  102.9 103.7 %collective-permute-start.12 = (bf16[1,64,1,128]{3,1,2,0:T(8,128)(2,1)S(1)}, bf16[1,64,1,128]{3,1,2,0:T(8,128)(2,1)S(1)}, u32[]{:S(2)}, u32[]{:S(2)}) collective-permute-start(bf16[1,64,1,128]{3,1,2,0:T(8,128)(2,1)S(1)} %bitcast.254), channel_id=1, source_target_pairs={{0,32},{32,64},{64,96},{96,128},{128,160},{160,192},{192,224},{1,3... | collective-permute-start | bytes 49160 | tf_op jit(solution)/shard_map/ppermute | solution.py:12
  110.7 1.0 copy-start.8
  111.8 1.2 copy-start.14
  113.0 1.5 copy-start.17
  207.3 5.2 %collective-permute-start.15 = (bf16[1,64,34,1]{1,2,3,0:T(8,128)(2,1)S(1)}, bf16[1,64,34,1]{1,2,3,0:T(8,128)(2,1)S(1)}, u32[]{:S(2)}, u32[]{:S(2)}) collective-permute-start(bf16[1,64,34,1]{1,2,3,0:T(8,128)(2,1)S(1)} %copy.242), channel_id=1, source_target_pairs={{16,0},{17,1},{18,2},{19,3},{20,4},{21,5},{22,6},{23,7},{24,8},{25... | collective-permute-start | bytes 13064 | tf_op jit(solution)/shard_map/ppermute | solution.py:15
  210.7 3.1 collective-permute-start.14
  217.0 0.9 copy-start.19
  (11 other events, 8.5 us)
Sparse Core Ops, SparseCore 0:
  114.6 264.1 all-reduce.3
where the time goes:
time: 395 us; the launch traced here: 388 us
  waiting for transfers between devices  160 us (41%)
  blocking collectives  92.1 us (23%)
  starting transfers between devices  43.8 us (11%)
  local copies, waits for them, and re-layouts  43.4 us (11%)
  matrix products  23.5 us (6%)
  between operations  15.1 us (4%)
  other arithmetic  10.2 us (3%)
    psum x1, waiting for transfers between devices, local(): lax.psum((grad_one, bias_grad_one, grad_two, bias_grad_two), ('sy', 'sx',...  156 us
    psum x1, blocking collectives, local(): lax.psum((grad_one, bias_grad_one, grad_two, bias_grad_two), ('sy', 'sx',...  92.1 us
    unnamed x67, local copies, waits for them, and re-layouts  30.3 us
    ppermute x8, starting transfers between devices, extended(): lax.ppermute(lax.slice_in_dim(block, block.shape[dim] - width, None, axis...  25.5 us
    ppermute x8, starting transfers between devices, extended(): lax.ppermute(lax.slice_in_dim(block, 0, width, axis=dim), axis, backward)  18.3 us
    dot_general x18, matrix products, kernel_grad(): jnp.einsum('ihw,ohw->io', window, delta[0], preferred_element_type=jnp.fl...  11.8 us
    conv_general_dilated x4, matrix products, convolve(): lax.conv_general_dilated(padded, kernel, (1, 1), 'VALID', dimension_numbe...  11.8 us
  transfers between devices with their start and end apart: 17, of which 4 were waited for; matrix products, arithmetic and copies ran while one was open for 10% of the time, Pallas kernels for 0%

commit v1 on v0

v1 whole, which is shorter than its diff:
```python
import functools

import jax
import jax.numpy as jnp
from jax import lax
from jax.experimental import pallas as pl
from jax.experimental.pallas import tpu as pltpu
from jax.sharding import PartitionSpec as P

BF = jnp.bfloat16
F32 = jnp.float32
MESH = pl.DeviceIdType.MESH
CH = 64
RB = 32
CB = 128
RW = 16
CW = 256
FLAT = 289


def sigmoid(x):
    return 0.5 * jnp.tanh(0.5 * x) + 0.5


def store_shifted(x, dst, r, lane):
    z = jnp.zeros_like(x)
    dst[r, 0:CH] = jnp.where(lane == 0, z, pltpu.roll(x, 1, 1))
    dst[r, CH : 2 * CH] = x
    dst[r, 2 * CH : 3 * CH] = jnp.where(lane == CW - 1, z, pltpu.roll(x, CW - 1, 1))


def build_weights(w_ref, dst, transposed):
    dst[...] = jnp.zeros_like(dst)
    for a in range(3):
        for b in range(3):
            if transposed:
                block = w_ref[2 - a, 2 - b]
            else:
                block = w_ref[a, b].astype(F32).T.astype(BF)
            for t in range(2):
                first = (a + t) * 3 * CH + b * CH
                dst[t * CH : (t + 1) * CH, first : first + CH] = block


def conv(w, src, k):
    rhs = src[pl.ds(2 * k, 4)].reshape(4 * 3 * CH, CW)
    return jnp.dot(w[...], rhs, preferred_element_type=F32)


def kernel(
    n_sy,
    n_grp,
    scale,
    x_ref,
    ct_ref,
    w1_ref,
    b1_ref,
    w2_ref,
    b2_ref,
    out_ref,
    ig_ref,
    g1_ref,
    gb1_ref,
    g2_ref,
    gb2_ref,
    turn,
    xt,
    ctt,
    xw,
    ctw,
    x3,
    h3,
    d3,
    e3,
    s1,
    dz,
    w1t,
    w2t,
    w1f,
    w2f,
    outw,
    igw,
    outs,
    igs,
    gacc,
    flat,
    part2,
    part1,
    in2,
    in1,
    mid2,
    mid1,
    fin2,
    fin1,
    send_halo,
    recv_halo,
    send_red,
    recv_red,
):
    sy = lax.axis_index("sy")
    sx = lax.axis_index("sx")
    grp = lax.axis_index("grp")
    n_m = 2 * n_sy
    m = sy * 2 + sx
    chunk = part1.shape[1]

    barrier = pltpu.get_barrier_semaphore()

    @pl.loop(1, n_m)
    def _(d):
        peer = lax.rem(m + d, n_m)
        pl.semaphore_signal(
            barrier,
            inc=1,
            device_id={"sy": peer // 2, "sx": lax.rem(peer, 2)},
            device_id_type=MESH,
        )

    @pl.loop(1, n_grp)
    def _(d):
        pl.semaphore_signal(
            barrier, inc=1, device_id={"grp": lax.rem(grp + d, n_grp)}, device_id_type=MESH
        )

    lane = lax.broadcasted_iota(jnp.int32, (CH, CW), 1)
    mine = pl.multiple_of(sx * CB, CB)
    other = pl.multiple_of((1 - sx) * CB, CB)

    def rows_major(src, dst):
        @pl.loop(0, 8)
        def _(c):
            part = src[pl.ds(8 * c, 8)].astype(F32).reshape(8 * RB, CB)
            turn[pl.ds(pl.multiple_of(8 * RB * c, 8 * RB), 8 * RB)] = part

        @pl.loop(0, RB)
        def _(r):
            dst[r] = turn[pl.ds(r, CH, stride=RB), :].astype(BF)

    def halo_copies(i, blk, win, width):
        span = RW + width
        near = pltpu.make_async_copy(
            blk.at[pl.ds(sx * (RW - width), span)],
            win.at[pl.ds((1 - sx) * width, span), :, pl.ds(mine, CB)],
            send_halo.at[i, 0],
        )
        pair = pltpu.make_async_remote_copy(
            src_ref=blk.at[pl.ds((1 - sx) * (RW - width), span)],
            dst_ref=win.at[pl.ds(sx * width, span), :, pl.ds(mine, CB)],
            send_sem=send_halo.at[i, 1],
            recv_sem=recv_halo.at[i, 0],
            device_id={"sx": 1 - sx},
            device_id_type=MESH,
        )
        down = pltpu.make_async_remote_copy(
            src_ref=blk.at[pl.ds(RB - width, width)],
            dst_ref=win.at[pl.ds(0, width), :, pl.ds(mine, CB)],
            send_sem=send_halo.at[i, 2],
            recv_sem=recv_halo.at[i, 1 + sx],
            device_id={"sy": sy + 1, "sx": 0},
            device_id_type=MESH,
        )
        up = pltpu.make_async_remote_copy(
            src_ref=blk.at[pl.ds(0, width)],
            dst_ref=win.at[pl.ds(RW + width, width), :, pl.ds(mine, CB)],
            send_sem=send_halo.at[i, 3],
            recv_sem=recv_halo.at[i, 1 + sx],
            device_id={"sy": sy - 1, "sx": 1},
            device_id_type=MESH,
        )
        return near, pair, down, up

    has_down = sy < n_sy - 1
    has_up = sy > 0
    takes = ((sx == 0) & has_up) | ((sx == 1) & has_down)

    def halo_start(i, blk, win, width):
        near, pair, down, up = halo_copies(i, blk, win, width)
        near.start()
        pair.start()
        pl.when(has_down)(down.start)
        pl.when(has_up)(up.start)
        empty = jnp.zeros((width, CH, CW), BF)

        @pl.when((sx == 0) & (sy == 0))
        def _():
            win[0:width] = empty

        @pl.when((sx == 1) & (sy == n_sy - 1))
        def _():
            win[RW + width : RW + 2 * width] = empty

    def halo_wait(i, blk, win, width):
        near, pair, down, up = halo_copies(i, blk, win, width)
        near.wait()
        pair.wait()
        pl.when(has_down)(down.wait_send)
        pl.when(has_up)(up.wait_send)

        @pl.when(takes)
        def _():
            for half in range(2):
                pltpu.make_async_remote_copy(
                    src_ref=blk.at[pl.ds(0, width)],
                    dst_ref=win.at[
                        pl.ds(sx * (RW + width), width), :, half * CB : (half + 1) * CB
                    ],
                    send_sem=send_halo.at[i, 2],
                    recv_sem=recv_halo.at[i, 1 + half],
                    device_id={"sx": 1 - sx},
                    device_id_type=MESH,
                ).wait_recv()

    rows_major(x_ref, xt)
    pl.semaphore_wait(barrier, n_m - 1 + n_grp - 1)
    halo_start(0, xt, xw, 4)
    rows_major(ct_ref, ctt)
    halo_start(1, ctt, ctw, 2)

    build_weights(w1_ref, w1t, False)
    build_weights(w2_ref, w2t, False)
    build_weights(w1_ref, w1f, True)
    build_weights(w2_ref, w2f, True)
    b1 = jnp.broadcast_to(b1_ref[...], (CH, CW))
    b2 = jnp.broadcast_to(b2_ref[...], (CH, CW))
    b1 = jnp.concatenate([b1, b1], 0)
    b2 = jnp.concatenate([b2, b2], 0)
    blank = jnp.zeros((CH, CW), BF)
    for r in (0, 1, RW + 2, RW + 3):
        dz[r] = blank
    first = (sx == 0) & (sy == 0)
    last = (sx == 1) & (sy == n_sy - 1)

    halo_wait(0, xt, xw, 4)

    @pl.loop(0, RW + 8)
    def _(r):
        store_shifted(xw[r], x3, r, lane)

    @pl.loop(0, (RW + 6) // 2)
    def _(k):
        pre = conv(w1t, x3, k) + b1
        gate = sigmoid(pre)
        h = (pre * gate).astype(BF)
        s1[pl.ds(2 * k, 2)] = (gate * (1.0 + pre * (1.0 - gate))).reshape(2, CH, CW)
        store_shifted(h[0:CH], h3, 2 * k, lane)
        store_shifted(h[CH : 2 * CH], h3, 2 * k + 1, lane)

    @pl.when(first)
    def _():
        h3[0:3] = jnp.zeros((3, 3 * CH, CW), BF)

    @pl.when(last)
    def _():
        h3[RW + 3 : RW + 6] = jnp.zeros((3, 3 * CH, CW), BF)

    halo_wait(1, ctt, ctw, 2)

    @pl.loop(0, (RW + 4) // 2)
    def _(k):
        pre = conv(w2t, h3, k) + b2
        gate = sigmoid(pre)
        slope = gate * (1.0 + pre * (1.0 - gate))
        ct = ctw[pl.ds(2 * k, 2)].reshape(2 * CH, CW)
        d = (ct.astype(F32) * slope).astype(BF)
        store_shifted(d[0:CH], d3, 2 * k, lane)
        store_shifted(d[CH : 2 * CH], d3, 2 * k + 1, lane)

        @pl.when((k > 0) & (k < (RW + 4) // 2 - 1))
        def _():
            outw[pl.ds(2 * k - 2, 2)] = (pre * gate).astype(BF).reshape(2, CH, CW)
            dz[pl.ds(2 * k, 2)] = d.reshape(2, CH, CW)

    def pair_copy(i, src, dst):
        return pltpu.make_async_remote_copy(
            src_ref=src.at[:, :, pl.ds(other, CB)],
            dst_ref=dst,
            send_sem=send_halo.at[2 + i, 0],
            recv_sem=recv_halo.at[2 + i, 0],
            device_id={"sx": 1 - sx},
            device_id_type=MESH,
        )

    pair_copy(0, outw, outs).start()

    def kernel_grad(src, off, dst):
        gacc[...] = jnp.zeros_like(gacc)
        ones = jnp.ones((16, CW), BF)

        @pl.loop(0, (RW + 2) // 2)
        def _(k):
            q = 2 * k
            left = [jnp.concatenate([src[q + j + off], ones], 0) for j in range(2)]
            right = [dz[pl.ds(q + j, 3)].reshape(3 * CH, CW) for j in range(2)]
            gacc[...] += lax.dot_general(
                jnp.concatenate(left, 1),
                jnp.concatenate(right, 1),
                (((1,), (1,)), ((), ())),
                preferred_element_type=F32,
            )

        flat[0:192] = gacc[0:192, 0:128]
        tail = gacc[0:192, 128:192]
        flat[192:288] = jnp.concatenate([tail[0:96], tail[96:192]], 1)
        flat[288:289] = gacc[192:193, 0:128]
        for j in range(n_m):
            top = min(FLAT, (j + 1) * chunk)
            if top > j * chunk:
                dst[j, 0 : top - j * chunk] = flat[j * chunk : top]

    def peer_of(d):
        peer = lax.rem(m + d, n_m)
        return peer, {"sy": peer // 2, "sx": lax.rem(peer, 2)}

    def scatter(i, part, landing):
        def copy(d):
            peer, where = peer_of(d)
            return pltpu.make_async_remote_copy(
                src_ref=part.at[peer],
                dst_ref=landing.at[m],
                send_sem=send_red.at[i, d],
                recv_sem=recv_red.at[i, m],
                device_id=where,
                device_id_type=MESH,
            )

        return copy

    def across(i, mid):
        def copy(d):
            return pltpu.make_async_remote_copy(
                src_ref=mid.at[grp],
                dst_ref=mid.at[grp],
                send_sem=send_red.at[i, d],
                recv_sem=recv_red.at[i, grp],
                device_id={"grp": lax.rem(grp + d, n_grp)},
                device_id_type=MESH,
            )

        return copy

    def gather(i, fin):
        def copy(d):
            _, where = peer_of(d)
            return pltpu.make_async_remote_copy(
                src_ref=fin.at[m],
                dst_ref=fin.at[m],
                send_sem=send_red.at[i, d],
                recv_sem=recv_red.at[i, m],
                device_id=where,
                device_id_type=MESH,
            )

        return copy

    def start_all(copy, count):
        @pl.loop(1, count)
        def _(d):
            copy(d).start()

    def wait_all(copy, i, count, me, landing):
        @pl.loop(1, count)
        def _(d):
            slot = lax.rem(me + d, count)
            copy(d).wait_send()
            pltpu.make_async_remote_copy(
                src_ref=landing.at[slot],
                dst_ref=landing.at[slot],
                send_sem=send_red.at[i, d],
                recv_sem=recv_red.at[i, slot],
                device_id={"sx": 1 - sx},
                device_id_type=MESH,
            ).wait_recv()

    def total(landing, count):
        acc = landing[0]
        for j in range(1, count):
            acc = acc + landing[j]
        return acc

    def step_scatter(i, part, landing):
        landing[m] = part[m]
        start_all(scatter(i, part, landing), n_m)

    def step_across(i, part, landing, mid):
        wait_all(scatter(i, part, landing), i, n_m, m, landing)
        mid[grp] = total(landing, n_m)
        start_all(across(i + 1, mid), n_grp)

    def step_gather(i, mid, fin):
        wait_all(across(i + 1, mid), i + 1, n_grp, grp, mid)
        fin[m] = total(mid, n_grp)
        start_all(gather(i + 2, fin), n_m)

    def step_end(i, fin, g_out, gb_out):
        wait_all(gather(i + 2, fin), i + 2, n_m, m, fin)
        for j in range(n_m):
            top = min(FLAT, (j + 1) * chunk)
            if top > j * chunk:
                flat[j * chunk : top] = fin[j, 0 : top - j * chunk] * scale
        wide = flat[0:192]
        g_out[2] = wide[:, 0:64]
        g_out[1] = wide[:, 64:128]
        tail = flat[192:288]
        g_out[0, 0:96] = tail[:, 0:64]
        g_out[0, 96:192] = tail[:, 64:128]
        gb_out[...] = flat[288:289, 0:64]

    kernel_grad(h3, 2, part2)
    step_scatter(0, part2, in2)

    @pl.loop(0, (RW + 2) // 2)
    def _(k):
        hg = conv(w2f, d3, k)
        d = (hg * s1[pl.ds(2 * k + 2, 2)].reshape(2 * CH, CW)).astype(BF)
        top, low = d[0:CH], d[CH : 2 * CH]
        store_shifted(top, e3, 2 * k, lane)
        store_shifted(low, e3, 2 * k + 1, lane)
        dz[2 * k + 1] = top
        dz[2 * k + 2] = low

    dz[1] = blank
    dz[RW + 2] = blank

    @pl.when(first)
    def _():
        e3[0] = jnp.zeros((3 * CH, CW), BF)

    @pl.when(last)
    def _():
        e3[RW + 1] = jnp.zeros((3 * CH, CW), BF)

    kernel_grad(x3, 3, part1)
    step_scatter(3, part1, in1)
    step_across(0, part2, in2, mid2)

    @pl.loop(0, RW // 2)
    def _(k):
        igw[pl.ds(2 * k, 2)] = conv(w1f, e3, k).astype(BF).reshape(2, CH, CW)

    pair_copy(1, igw, igs).start()
    step_across(3, part1, in1, mid1)
    step_gather(0, mid2, fin2)

    def channels_major(i, own, got, dst):
        pair_copy(i, own, got).wait()

        @pl.loop(0, RW)
        def _(r):
            turn[pl.ds(sx * RW + r, CH, stride=RB), :] = own[r, :, pl.ds(mine, CB)].astype(F32)
            turn[pl.ds((1 - sx) * RW + r, CH, stride=RB), :] = got[r].astype(F32)

        @pl.loop(0, 8)
        def _(c):
            part = turn[pl.ds(pl.multiple_of(8 * RB * c, 8 * RB), 8 * RB)]
            dst[pl.ds(8 * c, 8)] = part.reshape(8, RB, CB).astype(BF)

    channels_major(0, outw, outs, out_ref)
    channels_major(1, igw, igs, ig_ref)
    step_gather(3, mid1, fin1)
    step_end(0, fin2, g2_ref, gb2_ref)
    step_end(3, fin1, g1_ref, gb1_ref)


def solution(mesh):
    n_sy = mesh.shape["sy"]
    n_grp = mesh.shape["grp"]
    n_m = 2 * n_sy
    chunk = -(-FLAT // n_m)
    scale = float((n_grp * n_sy * RB * 2 * CB) ** -0.5)
    most = max(n_m, n_grp)
    call = pl.pallas_call(
        functools.partial(kernel, n_sy, n_grp, scale),
        out_shape=[
            jax.ShapeDtypeStruct((CH, RB, CB), BF),
            jax.ShapeDtypeStruct((CH, RB, CB), BF),
            jax.ShapeDtypeStruct((3, 3 * CH, CH), F32),
            jax.ShapeDtypeStruct((1, CH), F32),
            jax.ShapeDtypeStruct((3, 3 * CH, CH), F32),
            jax.ShapeDtypeStruct((1, CH), F32),
        ],
        in_specs=[pl.BlockSpec(memory_space=pltpu.VMEM)] * 6,
        out_specs=[pl.BlockSpec(memory_space=pltpu.VMEM)] * 6,
        scratch_shapes=[
            pltpu.VMEM((CH * RB, CB), F32),
            pltpu.VMEM((RB, CH, CB), BF),
            pltpu.VMEM((RB, CH, CB), BF),
            pltpu.VMEM((RW + 8, CH, CW), BF),
            pltpu.VMEM((RW + 4, CH, CW), BF),
            pltpu.VMEM((RW + 8, 3 * CH, CW), BF),
            pltpu.VMEM((RW + 6, 3 * CH, CW), BF),
            pltpu.VMEM((RW + 4, 3 * CH, CW), BF),
            pltpu.VMEM((RW + 2, 3 * CH, CW), BF),
            pltpu.VMEM((RW + 6, CH, CW), F32),
            pltpu.VMEM((RW + 4, CH, CW), BF),
            pltpu.VMEM((2 * CH, 12 * CH), BF),
            pltpu.VMEM((2 * CH, 12 * CH), BF),
            pltpu.VMEM((2 * CH, 12 * CH), BF),
            pltpu.VMEM((2 * CH, 12 * CH), BF),
            pltpu.VMEM((RW, CH, CW), BF),
            pltpu.VMEM((RW, CH, CW), BF),
            pltpu.VMEM((RW, CH, CB), BF),
            pltpu.VMEM((RW, CH, CB), BF),
            pltpu.VMEM((208, 192), F32),
            pltpu.VMEM((FLAT, 128), F32),
            pltpu.VMEM((n_m, chunk, 128), F32),
            pltpu.VMEM((n_m, chunk, 128), F32),
            pltpu.VMEM((n_m, chunk, 128), F32),
            pltpu.VMEM((n_m, chunk, 128), F32),
            pltpu.VMEM((n_grp, chunk, 128), F32),
            pltpu.VMEM((n_grp, chunk, 128), F32),
            pltpu.VMEM((n_m, chunk, 128), F32),
            pltpu.VMEM((n_m, chunk, 128), F32),
            pltpu.SemaphoreType.DMA((4, 4)),
            pltpu.SemaphoreType.DMA((4, 3)),
            pltpu.SemaphoreType.DMA((6, most)),
            pltpu.SemaphoreType.DMA((6, most)),
        ],
        compiler_params=pltpu.CompilerParams(
            collective_id=0, has_side_effects=True, vmem_limit_bytes=50 * 1024 * 1024
        ),
        name="blocks",
    )

    def local(image, weight_one, bias_one, weight_two, bias_two, cotangent):
        output, image_grad, g1, gb1, g2, gb2 = call(
            image[0],
            cotangent[0],
            weight_one,
            bias_one.reshape(CH, 1),
            weight_two,
            bias_two.reshape(CH, 1),
        )
        return (
            output[None],
            image_grad[None],
            g1.reshape(3, 3, CH, CH),
            gb1.reshape(CH),
            g2.reshape(3, 3, CH, CH),
            gb2.reshape(CH),
        )

    tile = P("grp", None, "sy", "sx")
    return jax.shard_map(
        local,
        mesh=mesh,
        in_specs=(tile, P(), P(), P(), P(), tile),
        out_specs=(tile, tile, P(), P(), P(), P()),
        check_vma=False,
    )
```

time: 395 us -> 61.5 us (0.16); the launches traced: 388 us -> 61.2 us
  waiting for transfers between devices: 160 us -> 0 us
  blocking collectives: 92.1 us -> 0 us
  Pallas kernels: 0 us -> 51.2 us
  starting transfers between devices: 43.8 us -> 0 us
  local copies, waits for them, and re-layouts: 43.4 us -> 9.34 us
  matrix products: 23.5 us -> 0 us
  between operations: 15.1 us -> 0.66 us
  other arithmetic: 10.2 us -> 0 us
    psum x1 -> x0, waiting for transfers between devices: 156 us -> none  [local(): lax.psum((grad_one, bias_grad_one, grad_two, bias_grad_two), ('sy', 'sx',...]
    psum x1 -> x0, blocking collectives: 92.1 us -> none  [local(): lax.psum((grad_one, bias_grad_one, grad_two, bias_grad_two), ('sy', 'sx',...]
    pallas_call x0 -> x1, Pallas kernels: none -> 51.2 us  [local(): call(image[0], cotangent[0], weight_one, bias_one.reshape(CH, 1), weight_...]
    ppermute x16 -> x0, starting transfers between devices: 43.8 us -> none  [the longest x8 25.5 us: extended(): lax.ppermute(lax.slice_in_dim(block, block.shape[dim] - width, None, axis...]
    unnamed x67 -> x18, local copies, waits for them, and re-layouts: 30.3 us -> 9.15 us
    dot_general x18 -> x0, matrix products: 11.8 us -> none  [kernel_grad(): jnp.einsum('ihw,ohw->io', window, delta[0], preferred_element_type=jnp.fl...]
    conv_general_dilated x4 -> x0, matrix products: 11.8 us -> none  [convolve(): lax.conv_general_dilated(padded, kernel, (1, 1), 'VALID', dimension_numbe...]
    concatenate x7 -> x0, other arithmetic: 6.63 us -> none  [extended(): block = jnp.concatenate([low, block, high], axis=dim)]
  transfers between devices with their start and end apart: 17 -> 0, of which waited for: 4 -> 0; matrix products, arithmetic and copies ran while one was open for 10% -> 0% of each run, Pallas kernels for 0% -> 0%
where the time goes in v1:
time: 61.5 us; the launch traced here: 61.2 us
  Pallas kernels  51.2 us (83%)
  local copies, waits for them, and re-layouts  9.34 us (15%)
  between operations  0.66 us (1%)
    pallas_call x1, Pallas kernels, local(): call(image[0], cotangent[0], weight_one, bias_one.reshape(CH, 1), weight_...  51.2 us
    unnamed x18, local copies, waits for them, and re-layouts  9.15 us

profile of v1, /device:TPU:1, one launch (start us, length us, event | category | flops | bytes accessed | tf_op | source)
XLA Modules:
  0.0 61.2 jit_solution(12441400728741569663)
XLA Ops:
  0.6 0.0 copy-start.4
  0.6 0.6 %copy-done.4 = f32[64]{0:T(128)S(1)} copy-done((f32[64]{0:T(128)S(1)}, f32[64]{0:T(128)}, u32[]{:S(2)}) %copy-start.4) | copy-done | bytes 280
  1.3 0.0 copy-start.5
  1.3 0.1 copy.12.b1_ref
  1.4 0.6 copy-done.5
  1.9 0.1 copy.13.b2_ref
  2.0 0.0 copy-start
  2.0 1.0 %copy-done = bf16[1,64,32,128]{3,2,1,0:T(8,128)(2,1)S(1)} copy-done((bf16[1,64,32,128]{3,2,1,0:T(8,128)(2,1)S(1)}, bf16[1,64,32,128]{3,2,1,0:T(8,128)(2,1)}, u32[]{:S(2)}) %copy-start) | copy-done | bytes 524312
  3.1 0.0 copy-start.1
  3.1 1.0 %copy-done.1 = bf16[1,64,32,128]{3,2,1,0:T(8,128)(2,1)S(1)} copy-done((bf16[1,64,32,128]{3,2,1,0:T(8,128)(2,1)S(1)}, bf16[1,64,32,128]{3,2,1,0:T(8,128)(2,1)}, u32[]{:S(2)}) %copy-start.1) | copy-done | bytes 524312
  4.1 0.0 copy-start.2
  4.1 0.9 %copy-done.2 = bf16[3,3,64,64]{3,2,1,0:T(8,128)(2,1)S(1)} copy-done((bf16[3,3,64,64]{3,2,1,0:T(8,128)(2,1)S(1)}, bf16[3,3,64,64]{3,2,1,0:T(8,128)(2,1)}, u32[]{:S(2)}) %copy-start.2) | copy-done | bytes 73752
  5.0 0.0 copy-start.3
  5.0 0.9 %copy-done.3 = bf16[3,3,64,64]{3,2,1,0:T(8,128)(2,1)S(1)} copy-done((bf16[3,3,64,64]{3,2,1,0:T(8,128)(2,1)S(1)}, bf16[3,3,64,64]{3,2,1,0:T(8,128)(2,1)}, u32[]{:S(2)}) %copy-start.3) | copy-done | bytes 73752
  5.9 51.2 %blocks.1 = (bf16[64,32,128]{2,1,0:T(8,128)(2,1)S(1)}, bf16[64,32,128]{2,1,0:T(8,128)(2,1)S(1)}, f32[3,192,64]{2,1,0:T(8,128)S(1)}, f32[1,64]{1,0:T(1,128)S(1)},...) custom-call(bf16[64,32,128]{2,1,0:T(8,128)(2,1)S(1)} %bitcast.12, bf16[64,32,128]{2,1,0:T(8,128)(2,1)S(1)} %bitcast.13, ...), custom_call_target="tpu_custom_call" | custom-call | tf_op jit(solution)/shard_map/blocks/pallas_call | solution.py:525
  57.2 0.8 %copy.20 = bf16[1,64,32,128]{3,2,1,0:T(8,128)(2,1)} copy(bf16[1,64,32,128]{3,2,1,0:T(8,128)(2,1)S(1)} %bitcast.11) | data formatting | bytes 1048576
  58.0 0.8 %copy.21 = bf16[1,64,32,128]{3,2,1,0:T(8,128)(2,1)} copy(bf16[1,64,32,128]{3,2,1,0:T(8,128)(2,1)S(1)} %bitcast.10) | data formatting | bytes 1048576
  58.8 0.7 %copy.22 = f32[3,3,64,64]{3,2,1,0:T(8,128)} copy(f32[3,3,64,64]{3,2,1,0:T(8,128)S(1)} %bitcast.15) | data formatting | bytes 294912
  59.5 0.5 copy.23
  60.0 0.7 %copy.24 = f32[3,3,64,64]{3,2,1,0:T(8,128)} copy(f32[3,3,64,64]{3,2,1,0:T(8,128)S(1)} %bitcast.14) | data formatting | bytes 294912
  60.7 0.5 copy.25
Async XLA Ops:
  0.6 0.7 %copy-start.4 = (f32[64]{0:T(128)S(1)}, f32[64]{0:T(128)}, u32[]{:S(2)}) copy-start(f32[64]{0:T(128)} %param.8) | copy-start | bytes 772
  1.3 0.7 %copy-start.5 = (f32[64]{0:T(128)S(1)}, f32[64]{0:T(128)}, u32[]{:S(2)}) copy-start(f32[64]{0:T(128)} %param.10) | copy-start | bytes 772
  2.0 1.0 %copy-start = (bf16[1,64,32,128]{3,2,1,0:T(8,128)(2,1)S(1)}, bf16[1,64,32,128]{3,2,1,0:T(8,128)(2,1)}, u32[]{:S(2)}) copy-start(bf16[1,64,32,128]{3,2,1,0:T(8,128)(2,1)} %param.6) | copy-start | bytes 1572868
  3.1 1.0 %copy-start.1 = (bf16[1,64,32,128]{3,2,1,0:T(8,128)(2,1)S(1)}, bf16[1,64,32,128]{3,2,1,0:T(8,128)(2,1)}, u32[]{:S(2)}) copy-start(bf16[1,64,32,128]{3,2,1,0:T(8,128)(2,1)} %param.11) | copy-start | bytes 1572868
  4.1 0.9 %copy-start.2 = (bf16[3,3,64,64]{3,2,1,0:T(8,128)(2,1)S(1)}, bf16[3,3,64,64]{3,2,1,0:T(8,128)(2,1)}, u32[]{:S(2)}) copy-start(bf16[3,3,64,64]{3,2,1,0:T(8,128)(2,1)} %w1_ref.1) | copy-start | bytes 221188
  5.0 0.9 %copy-start.3 = (bf16[3,3,64,64]{3,2,1,0:T(8,128)(2,1)S(1)}, bf16[3,3,64,64]{3,2,1,0:T(8,128)(2,1)}, u32[]{:S(2)}) copy-start(bf16[3,3,64,64]{3,2,1,0:T(8,128)(2,1)} %w2_ref.1) | copy-start | bytes 221188

commit v2 on v1

--- a/solution.py
+++ b/solution.py
@@ -51,18 +51,24 @@
     n_sy,
     n_grp,
     scale,
+    x_hbm,
+    ct_hbm,
+    w1_hbm,
+    b1_hbm,
+    w2_hbm,
+    b2_hbm,
+    out_ref,
+    ig_ref,
+    g1_ref,
+    gb1_ref,
+    g2_ref,
+    gb2_ref,
     x_ref,
     ct_ref,
     w1_ref,
     b1_ref,
     w2_ref,
     b2_ref,
-    out_ref,
-    ig_ref,
-    g1_ref,
-    gb1_ref,
-    g2_ref,
-    gb2_ref,
     turn,
     xt,
     ctt,
@@ -96,6 +102,7 @@
     recv_halo,
     send_red,
     recv_red,
+    load_sem,
 ):
     sy = lax.axis_index("sy")
     sx = lax.axis_index("sx")
@@ -103,6 +110,18 @@
     n_m = 2 * n_sy
     m = sy * 2 + sx
     chunk = part1.shape[1]
+
+    loads = [
+        pltpu.make_async_copy(src.at[part], dst.at[part], load_sem.at[i])
+        for i, (src, dst, part) in enumerate(
+            [(x_hbm, x_ref, pl.ds(16 * j, 16)) for j in range(4)]
+            + [(ct_hbm, ct_ref, pl.ds(16 * j, 16)) for j in range(4)]
+            + [(src, dst, pl.ds(0, src.shape[0])) for src, dst in (
+                (w1_hbm, w1_ref), (w2_hbm, w2_ref), (b1_hbm, b1_ref), (b2_hbm, b2_ref))]
+        )
+    ]
+    for load in loads:
+        load.start()
 
     barrier = pltpu.get_barrier_semaphore()
 
@@ -126,32 +145,39 @@
     mine = pl.multiple_of(sx * CB, CB)
     other = pl.multiple_of((1 - sx) * CB, CB)
 
-    def rows_major(src, dst):
-        @pl.loop(0, 8)
-        def _(c):
-            part = src[pl.ds(8 * c, 8)].astype(F32).reshape(8 * RB, CB)
-            turn[pl.ds(pl.multiple_of(8 * RB * c, 8 * RB), 8 * RB)] = part
-
-        @pl.loop(0, RB)
+    def rows_major(first, src, dst):
+        for j in range(4):
+            loads[first + j].wait()
+            part = src[16 * j : 16 * j + 16].astype(F32).reshape(16 * RB, CB)
+            turn[16 * RB * j : 16 * RB * (j + 1)] = part
+
+        @pl.loop(0, RB, unroll=RB)
         def _(r):
             dst[r] = turn[pl.ds(r, CH, stride=RB), :].astype(BF)
 
-    def halo_copies(i, blk, win, width):
-        span = RW + width
-        near = pltpu.make_async_copy(
-            blk.at[pl.ds(sx * (RW - width), span)],
-            win.at[pl.ds((1 - sx) * width, span), :, pl.ds(mine, CB)],
+    has_down = sy < n_sy - 1
+    has_up = sy > 0
+    takes = ((sx == 0) & has_up) | ((sx == 1) & has_down)
+
+    def halo_near(i, blk, win, width):
+        return pltpu.make_async_copy(
+            blk.at[pl.ds(sx * (RW - width), RW + width)],
+            win.at[pl.ds((1 - sx) * width, RW + width), :, pl.ds(mine, CB)],
             send_halo.at[i, 0],
         )
-        pair = pltpu.make_async_remote_copy(
-            src_ref=blk.at[pl.ds((1 - sx) * (RW - width), span)],
-            dst_ref=win.at[pl.ds(sx * width, span), :, pl.ds(mine, CB)],
+
+    def halo_pair(i, blk, win, width):
+        return pltpu.make_async_remote_copy(
+            src_ref=blk.at[pl.ds((1 - sx) * (RW - width), RW + width)],
+            dst_ref=win.at[pl.ds(sx * width, RW + width), :, pl.ds(mine, CB)],
             send_sem=send_halo.at[i, 1],
             recv_sem=recv_halo.at[i, 0],
             device_id={"sx": 1 - sx},
             device_id_type=MESH,
         )
-        down = pltpu.make_async_remote_copy(
+
+    def halo_down(i, blk, win, width):
+        return pltpu.make_async_remote_copy(
             src_ref=blk.at[pl.ds(RB - width, width)],
             dst_ref=win.at[pl.ds(0, width), :, pl.ds(mine, CB)],
             send_sem=send_halo.at[i, 2],
@@ -159,7 +185,9 @@
             device_id={"sy": sy + 1, "sx": 0},
             device_id_type=MESH,
         )
-        up = pltpu.make_async_remote_copy(
+
+    def halo_up(i, blk, win, width):
+        return pltpu.make_async_remote_copy(
             src_ref=blk.at[pl.ds(0, width)],
             dst_ref=win.at[pl.ds(RW + width, width), :, pl.ds(mine, CB)],
             send_sem=send_halo.at[i, 3],
@@ -167,18 +195,13 @@
             device_id={"sy": sy - 1, "sx": 1},
             device_id_type=MESH,
         )
-        return near, pair, down, up
-
-    has_down = sy < n_sy - 1
-    has_up = sy > 0
-    takes = ((sx == 0) & has_up) | ((sx == 1) & has_down)
-
-    def halo_start(i, blk, win, width):
-        near, pair, down, up = halo_copies(i, blk, win, width)
-        near.start()
-        pair.start()
-        pl.when(has_down)(down.start)
-        pl.when(has_up)(up.start)
+
+    def halo_start(*what):
+        _, _, win, width = what
+        pl.when(has_down)(lambda: halo_down(*what).start())
+        pl.when(has_up)(lambda: halo_up(*what).start())
+        halo_pair(*what).start()
+        halo_near(*what).start()
         empty = jnp.zeros((width, CH, CW), BF)
 
         @pl.when((sx == 0) & (sy == 0))
@@ -189,12 +212,14 @@
         def _():
             win[RW + width : RW + 2 * width] = empty
 
-    def halo_wait(i, blk, win, width):
-        near, pair, down, up = halo_copies(i, blk, win, width)
-        near.wait()
-        pair.wait()
-        pl.when(has_down)(down.wait_send)
-        pl.when(has_up)(up.wait_send)
+    def halo_wait_pair(*what):
+        halo_near(*what).wait()
+        halo_pair(*what).wait()
+
+    def halo_wait_far(*what):
+        i, blk, win, width = what
+        pl.when(has_down)(lambda: halo_down(*what).wait_send())
+        pl.when(has_up)(lambda: halo_up(*what).wait_send())
 
         @pl.when(takes)
         def _():
@@ -210,34 +235,43 @@
                     device_id_type=MESH,
                 ).wait_recv()
 
-    rows_major(x_ref, xt)
+    rows_major(0, x_ref, xt)
     pl.semaphore_wait(barrier, n_m - 1 + n_grp - 1)
     halo_start(0, xt, xw, 4)
-    rows_major(ct_ref, ctt)
+    rows_major(4, ct_ref, ctt)
     halo_start(1, ctt, ctw, 2)
 
+    for load in loads[8:]:
+        load.wait()
     build_weights(w1_ref, w1t, False)
     build_weights(w2_ref, w2t, False)
     build_weights(w1_ref, w1f, True)
     build_weights(w2_ref, w2f, True)
-    b1 = jnp.broadcast_to(b1_ref[...], (CH, CW))
-    b2 = jnp.broadcast_to(b2_ref[...], (CH, CW))
-    b1 = jnp.concatenate([b1, b1], 0)
-    b2 = jnp.concatenate([b2, b2], 0)
+
+    def column(ref):
+        across_rows = jnp.broadcast_to(ref[...], (CH, CH))
+        one = jnp.where(
+            lax.broadcasted_iota(jnp.int32, (CH, CH), 0)
+            == lax.broadcasted_iota(jnp.int32, (CH, CH), 1),
+            across_rows,
+            0.0,
+        )
+        col = jnp.broadcast_to(jnp.sum(one, axis=1, keepdims=True), (CH, CW))
+        return jnp.concatenate([col, col], 0)
+
+    b1 = column(b1_ref)
+    b2 = column(b2_ref)
     blank = jnp.zeros((CH, CW), BF)
-    for r in (0, 1, RW + 2, RW + 3):
-        dz[r] = blank
     first = (sx == 0) & (sy == 0)
     last = (sx == 1) & (sy == n_sy - 1)
 
-    halo_wait(0, xt, xw, 4)
-
-    @pl.loop(0, RW + 8)
+    halo_wait_pair(0, xt, xw, 4)
+
+    @pl.loop(0, RW + 4, unroll=RW + 4)
     def _(r):
-        store_shifted(xw[r], x3, r, lane)
-
-    @pl.loop(0, (RW + 6) // 2)
-    def _(k):
+        store_shifted(xw[r + 4 - 4 * sx], x3, r + 4 - 4 * sx, lane)
+
+    def hidden_rows(k):
         pre = conv(w1t, x3, k) + b1
         gate = sigmoid(pre)
         h = (pre * gate).astype(BF)
@@ -245,6 +279,20 @@
         store_shifted(h[0:CH], h3, 2 * k, lane)
         store_shifted(h[CH : 2 * CH], h3, 2 * k + 1, lane)
 
+    @pl.loop(0, (RW + 2) // 2, unroll=(RW + 2) // 2)
+    def _(k):
+        hidden_rows(k + 2 - 2 * sx)
+
+    halo_wait_far(0, xt, xw, 4)
+
+    @pl.loop(0, 4, unroll=4)
+    def _(r):
+        store_shifted(xw[r + (RW + 4) * sx], x3, r + (RW + 4) * sx, lane)
+
+    @pl.loop(0, 2, unroll=2)
+    def _(k):
+        hidden_rows(k + (RW + 2) // 2 * sx)
+
     @pl.when(first)
     def _():
         h3[0:3] = jnp.zeros((3, 3 * CH, CW), BF)
@@ -253,9 +301,10 @@
     def _():
         h3[RW + 3 : RW + 6] = jnp.zeros((3, 3 * CH, CW), BF)
 
-    halo_wait(1, ctt, ctw, 2)
-
-    @pl.loop(0, (RW + 4) // 2)
+    halo_wait_pair(1, ctt, ctw, 2)
+    halo_wait_far(1, ctt, ctw, 2)
+
+    @pl.loop(0, (RW + 4) // 2, unroll=(RW + 4) // 2)
     def _(k):
         pre = conv(w2t, h3, k) + b2
         gate = sigmoid(pre)
@@ -265,10 +314,11 @@
         store_shifted(d[0:CH], d3, 2 * k, lane)
         store_shifted(d[CH : 2 * CH], d3, 2 * k + 1, lane)
 
-        @pl.when((k > 0) & (k < (RW + 4) // 2 - 1))
-        def _():
-            outw[pl.ds(2 * k - 2, 2)] = (pre * gate).astype(BF).reshape(2, CH, CW)
-            dz[pl.ds(2 * k, 2)] = d.reshape(2, CH, CW)
+        outw[pl.ds(2 * k, 2)] = (pre * gate).astype(BF).reshape(2, CH, CW)
+        dz[pl.ds(2 * k, 2)] = d.reshape(2, CH, CW)
+
+    for r in (0, 1, RW + 2, RW + 3):
+        dz[r] = blank
 
     def pair_copy(i, src, dst):
         return pltpu.make_async_remote_copy(
@@ -280,13 +330,13 @@
             device_id_type=MESH,
         )
 
-    pair_copy(0, outw, outs).start()
+    pair_copy(0, outw.at[pl.ds(2, RW)], outs).start()
 
     def kernel_grad(src, off, dst):
         gacc[...] = jnp.zeros_like(gacc)
         ones = jnp.ones((16, CW), BF)
 
-        @pl.loop(0, (RW + 2) // 2)
+        @pl.loop(0, (RW + 2) // 2, unroll=(RW + 2) // 2)
         def _(k):
             q = 2 * k
             left = [jnp.concatenate([src[q + j + off], ones], 0) for j in range(2)]
@@ -408,7 +458,7 @@
     kernel_grad(h3, 2, part2)
     step_scatter(0, part2, in2)
 
-    @pl.loop(0, (RW + 2) // 2)
+    @pl.loop(0, (RW + 2) // 2, unroll=(RW + 2) // 2)
     def _(k):
         hg = conv(w2f, d3, k)
         d = (hg * s1[pl.ds(2 * k + 2, 2)].reshape(2 * CH, CW)).astype(BF)
@@ -433,7 +483,7 @@
     step_scatter(3, part1, in1)
     step_across(0, part2, in2, mid2)
 
-    @pl.loop(0, RW // 2)
+    @pl.loop(0, RW // 2, unroll=RW // 2)
     def _(k):
         igw[pl.ds(2 * k, 2)] = conv(w1f, e3, k).astype(BF).reshape(2, CH, CW)
 
@@ -444,21 +494,32 @@
     def channels_major(i, own, got, dst):
         pair_copy(i, own, got).wait()
 
-        @pl.loop(0, RW)
+        @pl.loop(0, RW, unroll=RW)
         def _(r):
             turn[pl.ds(sx * RW + r, CH, stride=RB), :] = own[r, :, pl.ds(mine, CB)].astype(F32)
             turn[pl.ds((1 - sx) * RW + r, CH, stride=RB), :] = got[r].astype(F32)
 
-        @pl.loop(0, 8)
+        @pl.loop(0, 8, unroll=8)
         def _(c):
             part = turn[pl.ds(pl.multiple_of(8 * RB * c, 8 * RB), 8 * RB)]
             dst[pl.ds(8 * c, 8)] = part.reshape(8, RB, CB).astype(BF)
 
-    channels_major(0, outw, outs, out_ref)
+    channels_major(0, outw.at[pl.ds(2, RW)], outs, out_ref)
     channels_major(1, igw, igs, ig_ref)
     step_gather(3, mid1, fin1)
     step_end(0, fin2, g2_ref, gb2_ref)
     step_end(3, fin1, g1_ref, gb1_ref)
+
+
+def write_out(*refs):
+    n = (len(refs) - 1) // 2
+    copies = [
+        pltpu.make_async_copy(refs[i], refs[n + i], refs[-1].at[i]) for i in range(n)
+    ]
+    for copy in copies:
+        copy.start()
+    for copy in copies:
+        copy.wait()
 
 
 def solution(mesh):
@@ -468,19 +529,26 @@
     chunk = -(-FLAT // n_m)
     scale = float((n_grp * n_sy * RB * 2 * CB) ** -0.5)
     most = max(n_m, n_grp)
+    shapes = [
+        jax.ShapeDtypeStruct((CH, RB, CB), BF),
+        jax.ShapeDtypeStruct((CH, RB, CB), BF),
+        jax.ShapeDtypeStruct((3, 3 * CH, CH), F32),
+        jax.ShapeDtypeStruct((1, CH), F32),
+        jax.ShapeDtypeStruct((3, 3 * CH, CH), F32),
+        jax.ShapeDtypeStruct((1, CH), F32),
+    ]
     call = pl.pallas_call(
         functools.partial(kernel, n_sy, n_grp, scale),
-        out_shape=[
-            jax.ShapeDtypeStruct((CH, RB, CB), BF),
-            jax.ShapeDtypeStruct((CH, RB, CB), BF),
-            jax.ShapeDtypeStruct((3, 3 * CH, CH), F32),
-            jax.ShapeDtypeStruct((1, CH), F32),
-            jax.ShapeDtypeStruct((3, 3 * CH, CH), F32),
-            jax.ShapeDtypeStruct((1, CH), F32),
-        ],
-        in_specs=[pl.BlockSpec(memory_space=pltpu.VMEM)] * 6,
+        out_shape=shapes,
+        in_specs=[pl.BlockSpec(memory_space=pltpu.HBM)] * 6,
         out_specs=[pl.BlockSpec(memory_space=pltpu.VMEM)] * 6,
         scratch_shapes=[
+            pltpu.VMEM((CH, RB, CB), BF),
+            pltpu.VMEM((CH, RB, CB), BF),
+            pltpu.VMEM((3, 3, CH, CH), BF),
+            pltpu.VMEM((1, CH), F32),
+            pltpu.VMEM((3, 3, CH, CH), BF),
+            pltpu.VMEM((1, CH), F32),
             pltpu.VMEM((CH * RB, CB), F32),
             pltpu.VMEM((RB, CH, CB), BF),
             pltpu.VMEM((RB, CH, CB), BF),
@@ -496,7 +564,7 @@
             pltpu.VMEM((2 * CH, 12 * CH), BF),
             pltpu.VMEM((2 * CH, 12 * CH), BF),
             pltpu.VMEM((2 * CH, 12 * CH), BF),
-            pltpu.VMEM((RW, CH, CW), BF),
+            pltpu.VMEM((RW + 4, CH, CW), BF),
             pltpu.VMEM((RW, CH, CW), BF),
             pltpu.VMEM((RW, CH, CB), BF),
             pltpu.VMEM((RW, CH, CB), BF),
@@ -514,21 +582,38 @@
             pltpu.SemaphoreType.DMA((4, 3)),
             pltpu.SemaphoreType.DMA((6, most)),
             pltpu.SemaphoreType.DMA((6, most)),
+            pltpu.SemaphoreType.DMA((12,)),
         ],
         compiler_params=pltpu.CompilerParams(
             collective_id=0, has_side_effects=True, vmem_limit_bytes=50 * 1024 * 1024
         ),
         name="blocks",
     )
+    store = pl.pallas_call(
+        write_out,
+        out_shape=shapes,
+        in_specs=[pl.BlockSpec(memory_space=pl.ANY)] * 6,
+        out_specs=[pl.BlockSpec(memory_space=pltpu.HBM)] * 6,
+        scratch_shapes=[pltpu.SemaphoreType.DMA((6,))],
+        compiler_params=pltpu.CompilerParams(vmem_limit_bytes=1024 * 1024),
+        name="write_out",
+    )
 
     def local(image, weight_one, bias_one, weight_two, bias_two, cotangent):
-        output, image_grad, g1, gb1, g2, gb2 = call(
-            image[0],
-            cotangent[0],
-            weight_one,
-            bias_one.reshape(CH, 1),
-            weight_two,
-            bias_two.reshape(CH, 1),
+        output, image_grad, g1, gb1, g2, gb2 = store(
+            *call(
+                *(
+                    pltpu.with_memory_space_constraint(v, pltpu.HBM)
+                    for v in (
+                        image[0],
+                        cotangent[0],
+                        weight_one,
+                        bias_one.reshape(1, CH),
+                        weight_two,
+                        bias_two.reshape(1, CH),
+                    )
+                )
+            )
         )
         return (
             output[None],

time: 61.5 us -> 42.2 us (0.69)
  Pallas kernels: 51.2 us -> 41.5 us
  local copies, waits for them, and re-layouts: 9.34 us -> 0 us
    pallas_call x1 -> x2, Pallas kernels: 51.2 us -> 41.5 us  [the longest x1 40.3 us: local(): call(*(pltpu.with_memory_space_constraint(v, pltpu.HBM) for v in (image[0...]
    unnamed x18 -> x0, local copies, waits for them, and re-layouts: 9.15 us -> none
where the time goes in v2:
time: 42.2 us; the launch traced here: 42.1 us
  Pallas kernels  41.5 us (98%)
  between operations  0.64 us (2%)
    pallas_call x1, Pallas kernels, local(): call(*(pltpu.with_memory_space_constraint(v, pltpu.HBM) for v in (image[0...  40.3 us
    pallas_call x1, Pallas kernels, local(): store(*call(*(pltpu.with_memory_space_constraint(v, pltpu.HBM) for v in (...  1.22 us

profile of v2, /device:TPU:1, one launch (start us, length us, event | category | flops | bytes accessed | tf_op | source)
XLA Modules:
  0.0 42.1 jit_solution(18194166106224712139)
XLA Ops:
  0.6 40.3 %blocks.1 = (bf16[64,32,128]{2,1,0:T(8,128)(2,1)S(1)}, bf16[64,32,128]{2,1,0:T(8,128)(2,1)S(1)}, f32[3,192,64]{2,1,0:T(8,128)S(1)}, f32[1,64]{1,0:T(1,128)S(1)},...) custom-call(bf16[64,32,128]{2,1,0:T(8,128)(2,1)} %bitcast.10, bf16[64,32,128]{2,1,0:T(8,128)(2,1)} %bitcast.11, ...), custom_call_target="tpu_custom_call" | custom-call | tf_op jit(solution)/shard_map/blocks/pallas_call | solution.py:604
  40.9 1.2 %write_out.1 = (bf16[64,32,128]{2,1,0:T(8,128)(2,1)}, bf16[64,32,128]{2,1,0:T(8,128)(2,1)}, f32[3,192,64]{2,1,0:T(8,128)}, f32[1,64]{1,0:T(1,128)}, f32[3,192,64]{2,1,0:T(8,128)}, /*index=5*/f32[1,64]{1,0:T(1,128)}) custom-call(bf16[64,32,128]{2,1,0:T(8,128)(2,1)S(1)} %get-tuple-element.18.refs_0_, bf16[64,32,128]{2,1,0:T(8,128)(2,1)S(1)} %get-tuple-element.19.refs_1_, ...), custom_call_target="tpu_custom_call" | custom-call | tf_op jit(solution)/shard_map/write_out/pallas_call | solution.py:603

commit v3 on v2

--- a/solution.py
+++ b/solution.py
@@ -15,7 +15,7 @@
 CB = 128
 RW = 16
 CW = 256
-FLAT = 289
+FLAT = 296
 
 
 def sigmoid(x):
@@ -79,7 +79,8 @@
     d3,
     e3,
     s1,
-    dz,
+    dz2,
+    dz1,
     w1t,
     w2t,
     w1f,
@@ -90,14 +91,10 @@
     igs,
     gacc,
     flat,
-    part2,
-    part1,
-    in2,
-    in1,
-    mid2,
-    mid1,
-    fin2,
-    fin1,
+    part,
+    landed,
+    mid,
+    fin,
     send_halo,
     recv_halo,
     send_red,
@@ -107,38 +104,57 @@
     sy = lax.axis_index("sy")
     sx = lax.axis_index("sx")
     grp = lax.axis_index("grp")
-    n_m = 2 * n_sy
-    m = sy * 2 + sx
-    chunk = part1.shape[1]
+    n_y = n_sy // 2
+    n_a, n_b = 8 * n_y, n_grp // 2
+    z, x_lo = grp // 2, lax.rem(grp, 2)
+    a = ((sy // n_y * 2 + x_lo) * n_y + lax.rem(sy, n_y)) * 2 + sx
+    b = z
+    chunk = part.shape[1]
 
     loads = [
-        pltpu.make_async_copy(src.at[part], dst.at[part], load_sem.at[i])
-        for i, (src, dst, part) in enumerate(
+        pltpu.make_async_copy(src.at[piece], dst.at[piece], load_sem.at[i])
+        for i, (src, dst, piece) in enumerate(
             [(x_hbm, x_ref, pl.ds(16 * j, 16)) for j in range(4)]
             + [(ct_hbm, ct_ref, pl.ds(16 * j, 16)) for j in range(4)]
-            + [(src, dst, pl.ds(0, src.shape[0])) for src, dst in (
-                (w1_hbm, w1_ref), (w2_hbm, w2_ref), (b1_hbm, b1_ref), (b2_hbm, b2_ref))]
+            + [
+                (src, dst, pl.ds(0, src.shape[0]))
+                for src, dst in (
+                    (w1_hbm, w1_ref),
+                    (w2_hbm, w2_ref),
+                    (b1_hbm, b1_ref),
+                    (b2_hbm, b2_ref),
+                )
+            ]
         )
     ]
     for load in loads:
         load.start()
 
+    def at_a(p):
+        spot = p // 2
+        x = spot // n_y
+        return {
+            "sy": x // 2 * n_y + lax.rem(spot, n_y),
+            "sx": lax.rem(p, 2),
+            "grp": z * 2 + lax.rem(x, 2),
+        }
+
+    def at_b(p):
+        return {"grp": p * 2 + x_lo}
+
+    has_down = sy < n_sy - 1
+    has_up = sy > 0
+    takes = ((sx == 0) & has_up) | ((sx == 1) & has_down)
+
     barrier = pltpu.get_barrier_semaphore()
 
-    @pl.loop(1, n_m)
-    def _(d):
-        peer = lax.rem(m + d, n_m)
+    for d in range(1, n_b):
         pl.semaphore_signal(
-            barrier,
-            inc=1,
-            device_id={"sy": peer // 2, "sx": lax.rem(peer, 2)},
-            device_id_type=MESH,
-        )
-
-    @pl.loop(1, n_grp)
-    def _(d):
+            barrier, inc=1, device_id=at_b(lax.rem(b + d, n_b)), device_id_type=MESH
+        )
+    for d in range(1, n_a):
         pl.semaphore_signal(
-            barrier, inc=1, device_id={"grp": lax.rem(grp + d, n_grp)}, device_id_type=MESH
+            barrier, inc=1, device_id=at_a(lax.rem(a + d, n_a)), device_id_type=MESH
         )
 
     lane = lax.broadcasted_iota(jnp.int32, (CH, CW), 1)
@@ -154,10 +170,6 @@
         @pl.loop(0, RB, unroll=RB)
         def _(r):
             dst[r] = turn[pl.ds(r, CH, stride=RB), :].astype(BF)
-
-    has_down = sy < n_sy - 1
-    has_up = sy > 0
-    takes = ((sx == 0) & has_up) | ((sx == 1) & has_down)
 
     def halo_near(i, blk, win, width):
         return pltpu.make_async_copy(
@@ -236,7 +248,7 @@
                 ).wait_recv()
 
     rows_major(0, x_ref, xt)
-    pl.semaphore_wait(barrier, n_m - 1 + n_grp - 1)
+    pl.semaphore_wait(barrier, n_a - 1 + n_b - 1)
     halo_start(0, xt, xw, 4)
     rows_major(4, ct_ref, ctt)
     halo_start(1, ctt, ctw, 2)
@@ -265,11 +277,8 @@
     first = (sx == 0) & (sy == 0)
     last = (sx == 1) & (sy == n_sy - 1)
 
-    halo_wait_pair(0, xt, xw, 4)
-
-    @pl.loop(0, RW + 4, unroll=RW + 4)
-    def _(r):
-        store_shifted(xw[r + 4 - 4 * sx], x3, r + 4 - 4 * sx, lane)
+    def each(count, body):
+        pl.loop(0, count, unroll=count)(body)
 
     def hidden_rows(k):
         pre = conv(w1t, x3, k) + b1
@@ -279,33 +288,7 @@
         store_shifted(h[0:CH], h3, 2 * k, lane)
         store_shifted(h[CH : 2 * CH], h3, 2 * k + 1, lane)
 
-    @pl.loop(0, (RW + 2) // 2, unroll=(RW + 2) // 2)
-    def _(k):
-        hidden_rows(k + 2 - 2 * sx)
-
-    halo_wait_far(0, xt, xw, 4)
-
-    @pl.loop(0, 4, unroll=4)
-    def _(r):
-        store_shifted(xw[r + (RW + 4) * sx], x3, r + (RW + 4) * sx, lane)
-
-    @pl.loop(0, 2, unroll=2)
-    def _(k):
-        hidden_rows(k + (RW + 2) // 2 * sx)
-
-    @pl.when(first)
-    def _():
-        h3[0:3] = jnp.zeros((3, 3 * CH, CW), BF)
-
-    @pl.when(last)
-    def _():
-        h3[RW + 3 : RW + 6] = jnp.zeros((3, 3 * CH, CW), BF)
-
-    halo_wait_pair(1, ctt, ctw, 2)
-    halo_wait_far(1, ctt, ctw, 2)
-
-    @pl.loop(0, (RW + 4) // 2, unroll=(RW + 4) // 2)
-    def _(k):
+    def output_rows(k):
         pre = conv(w2t, h3, k) + b2
         gate = sigmoid(pre)
         slope = gate * (1.0 + pre * (1.0 - gate))
@@ -313,12 +296,52 @@
         d = (ct.astype(F32) * slope).astype(BF)
         store_shifted(d[0:CH], d3, 2 * k, lane)
         store_shifted(d[CH : 2 * CH], d3, 2 * k + 1, lane)
-
         outw[pl.ds(2 * k, 2)] = (pre * gate).astype(BF).reshape(2, CH, CW)
-        dz[pl.ds(2 * k, 2)] = d.reshape(2, CH, CW)
+        dz2[pl.ds(2 * k, 2)] = d.reshape(2, CH, CW)
+
+    def delta_rows(k):
+        hg = conv(w2f, d3, k)
+        d = (hg * s1[pl.ds(2 * k + 2, 2)].reshape(2 * CH, CW)).astype(BF)
+        top, low = d[0:CH], d[CH : 2 * CH]
+        store_shifted(top, e3, 2 * k, lane)
+        store_shifted(low, e3, 2 * k + 1, lane)
+        dz1[2 * k + 1] = top
+        dz1[2 * k + 2] = low
+
+    halo_wait_pair(0, xt, xw, 4)
+    each(RW + 4, lambda r: store_shifted(xw[r + 4 - 4 * sx], x3, r + 4 - 4 * sx, lane))
+    each(RW // 2 + 1, lambda k: hidden_rows(k + 2 - 2 * sx))
+    halo_wait_pair(1, ctt, ctw, 2)
+    each(RW // 2, lambda k: output_rows(k + 2 - 2 * sx))
+    each(RW // 2 - 1, lambda k: delta_rows(k + 2 - 2 * sx))
+
+    halo_wait_far(0, xt, xw, 4)
+    each(4, lambda r: store_shifted(xw[r + (RW + 4) * sx], x3, r + (RW + 4) * sx, lane))
+    each(2, lambda k: hidden_rows(k + (RW // 2 + 1) * sx))
+
+    @pl.when(first)
+    def _():
+        h3[0:3] = jnp.zeros((3, 3 * CH, CW), BF)
+
+    @pl.when(last)
+    def _():
+        h3[RW + 3 : RW + 6] = jnp.zeros((3, 3 * CH, CW), BF)
+
+    halo_wait_far(1, ctt, ctw, 2)
+    each(2, lambda k: output_rows(k + RW // 2 * sx))
+    each(2, lambda k: delta_rows(k + (RW // 2 - 1) * sx))
+
+    @pl.when(first)
+    def _():
+        e3[0] = jnp.zeros((3 * CH, CW), BF)
+
+    @pl.when(last)
+    def _():
+        e3[RW + 1] = jnp.zeros((3 * CH, CW), BF)
 
     for r in (0, 1, RW + 2, RW + 3):
-        dz[r] = blank
+        dz2[r] = blank
+        dz1[r] = blank
 
     def pair_copy(i, src, dst):
         return pltpu.make_async_remote_copy(
@@ -330,9 +353,8 @@
             device_id_type=MESH,
         )
 
-    pair_copy(0, outw.at[pl.ds(2, RW)], outs).start()
-
-    def kernel_grad(src, off, dst):
+
+    def kernel_grad(src, off, dz, base):
         gacc[...] = jnp.zeros_like(gacc)
         ones = jnp.ones((16, CW), BF)
 
@@ -348,78 +370,33 @@
                 preferred_element_type=F32,
             )
 
-        flat[0:192] = gacc[0:192, 0:128]
+        flat[base : base + 192] = gacc[0:192, 0:128]
         tail = gacc[0:192, 128:192]
-        flat[192:288] = jnp.concatenate([tail[0:96], tail[96:192]], 1)
-        flat[288:289] = gacc[192:193, 0:128]
-        for j in range(n_m):
-            top = min(FLAT, (j + 1) * chunk)
-            if top > j * chunk:
-                dst[j, 0 : top - j * chunk] = flat[j * chunk : top]
-
-    def peer_of(d):
-        peer = lax.rem(m + d, n_m)
-        return peer, {"sy": peer // 2, "sx": lax.rem(peer, 2)}
-
-    def scatter(i, part, landing):
-        def copy(d):
-            peer, where = peer_of(d)
-            return pltpu.make_async_remote_copy(
-                src_ref=part.at[peer],
-                dst_ref=landing.at[m],
-                send_sem=send_red.at[i, d],
-                recv_sem=recv_red.at[i, m],
-                device_id=where,
+        flat[base + 192 : base + 288] = jnp.concatenate([tail[0:96], tail[96:192]], 1)
+        flat[base + 288 : base + FLAT] = gacc[192:200, 0:128]
+
+    def send_parts(i, count, me, where, source, landing):
+        for d in range(1, count):
+            p = lax.rem(me + d, count)
+            pltpu.make_async_remote_copy(
+                src_ref=source(p),
+                dst_ref=landing.at[me],
+                send_sem=send_red.at[i],
+                recv_sem=recv_red.at[i],
+                device_id=where(p),
                 device_id_type=MESH,
-            )
-
-        return copy
-
-    def across(i, mid):
-        def copy(d):
-            return pltpu.make_async_remote_copy(
-                src_ref=mid.at[grp],
-                dst_ref=mid.at[grp],
-                send_sem=send_red.at[i, d],
-                recv_sem=recv_red.at[i, grp],
-                device_id={"grp": lax.rem(grp + d, n_grp)},
-                device_id_type=MESH,
-            )
-
-        return copy
-
-    def gather(i, fin):
-        def copy(d):
-            _, where = peer_of(d)
-            return pltpu.make_async_remote_copy(
-                src_ref=fin.at[m],
-                dst_ref=fin.at[m],
-                send_sem=send_red.at[i, d],
-                recv_sem=recv_red.at[i, m],
-                device_id=where,
-                device_id_type=MESH,
-            )
-
-        return copy
-
-    def start_all(copy, count):
-        @pl.loop(1, count)
-        def _(d):
-            copy(d).start()
-
-    def wait_all(copy, i, count, me, landing):
-        @pl.loop(1, count)
-        def _(d):
-            slot = lax.rem(me + d, count)
-            copy(d).wait_send()
-            pltpu.make_async_remote_copy(
-                src_ref=landing.at[slot],
-                dst_ref=landing.at[slot],
-                send_sem=send_red.at[i, d],
-                recv_sem=recv_red.at[i, slot],
-                device_id={"sx": 1 - sx},
-                device_id_type=MESH,
-            ).wait_recv()
+            ).start()
+
+    def wait_parts(i, count, landing):
+        rest = landing.at[pl.ds(0, count - 1)]
+        pltpu.make_async_remote_copy(
+            src_ref=rest,
+            dst_ref=rest,
+            send_sem=send_red.at[i],
+            recv_sem=recv_red.at[i],
+            device_id={"sx": 1 - sx},
+            device_id_type=MESH,
+        ).wait()
 
     def total(landing, count):
         acc = landing[0]
@@ -427,69 +404,14 @@
             acc = acc + landing[j]
         return acc
 
-    def step_scatter(i, part, landing):
-        landing[m] = part[m]
-        start_all(scatter(i, part, landing), n_m)
-
-    def step_across(i, part, landing, mid):
-        wait_all(scatter(i, part, landing), i, n_m, m, landing)
-        mid[grp] = total(landing, n_m)
-        start_all(across(i + 1, mid), n_grp)
-
-    def step_gather(i, mid, fin):
-        wait_all(across(i + 1, mid), i + 1, n_grp, grp, mid)
-        fin[m] = total(mid, n_grp)
-        start_all(gather(i + 2, fin), n_m)
-
-    def step_end(i, fin, g_out, gb_out):
-        wait_all(gather(i + 2, fin), i + 2, n_m, m, fin)
-        for j in range(n_m):
-            top = min(FLAT, (j + 1) * chunk)
-            if top > j * chunk:
-                flat[j * chunk : top] = fin[j, 0 : top - j * chunk] * scale
-        wide = flat[0:192]
+    def unpack(base, g_out, gb_out):
+        wide = flat[base : base + 192]
         g_out[2] = wide[:, 0:64]
         g_out[1] = wide[:, 64:128]
-        tail = flat[192:288]
+        tail = flat[base + 192 : base + 288]
         g_out[0, 0:96] = tail[:, 0:64]
         g_out[0, 96:192] = tail[:, 64:128]
-        gb_out[...] = flat[288:289, 0:64]
-
-    kernel_grad(h3, 2, part2)
-    step_scatter(0, part2, in2)
-
-    @pl.loop(0, (RW + 2) // 2, unroll=(RW + 2) // 2)
-    def _(k):
-        hg = conv(w2f, d3, k)
-        d = (hg * s1[pl.ds(2 * k + 2, 2)].reshape(2 * CH, CW)).astype(BF)
-        top, low = d[0:CH], d[CH : 2 * CH]
-        store_shifted(top, e3, 2 * k, lane)
-        store_shifted(low, e3, 2 * k + 1, lane)
-        dz[2 * k + 1] = top
-        dz[2 * k + 2] = low
-
-    dz[1] = blank
-    dz[RW + 2] = blank
-
-    @pl.when(first)
-    def _():
-        e3[0] = jnp.zeros((3 * CH, CW), BF)
-
-    @pl.when(last)
-    def _():
-        e3[RW + 1] = jnp.zeros((3 * CH, CW), BF)
-
-    kernel_grad(x3, 3, part1)
-    step_scatter(3, part1, in1)
-    step_across(0, part2, in2, mid2)
-
-    @pl.loop(0, RW // 2, unroll=RW // 2)
-    def _(k):
-        igw[pl.ds(2 * k, 2)] = conv(w1f, e3, k).astype(BF).reshape(2, CH, CW)
-
-    pair_copy(1, igw, igs).start()
-    step_across(3, part1, in1, mid1)
-    step_gather(0, mid2, fin2)
+        gb_out[...] = flat[base + 288 : base + 289, 0:64]
 
     def channels_major(i, own, got, dst):
         pair_copy(i, own, got).wait()
@@ -504,11 +426,36 @@
             part = turn[pl.ds(pl.multiple_of(8 * RB * c, 8 * RB), 8 * RB)]
             dst[pl.ds(8 * c, 8)] = part.reshape(8, RB, CB).astype(BF)
 
+    if n_a * chunk > 2 * FLAT:
+        flat[2 * FLAT :] = jnp.zeros((n_a * chunk - 2 * FLAT, 128), F32)
+    kernel_grad(x3, 3, dz1, 0)
+    kernel_grad(h3, 2, dz2, FLAT)
+    for j in range(n_a):
+        part[j] = flat[j * chunk : (j + 1) * chunk]
+    send_parts(0, n_a, a, at_a, lambda p: part.at[p], landed)
+    landed[a] = part[a]
+    pair_copy(0, outw.at[pl.ds(2, RW)], outs).start()
+
+    @pl.loop(0, RW // 2, unroll=RW // 2)
+    def _(k):
+        igw[pl.ds(2 * k, 2)] = conv(w1f, e3, k).astype(BF).reshape(2, CH, CW)
+
+    pair_copy(1, igw, igs).start()
     channels_major(0, outw.at[pl.ds(2, RW)], outs, out_ref)
+
+    wait_parts(0, n_a, landed)
+    mid[b] = total(landed, n_a)
+    send_parts(1, n_b, b, at_b, lambda p: mid.at[b], mid)
     channels_major(1, igw, igs, ig_ref)
-    step_gather(3, mid1, fin1)
-    step_end(0, fin2, g2_ref, gb2_ref)
-    step_end(3, fin1, g1_ref, gb1_ref)
+
+    wait_parts(1, n_b, mid)
+    fin[a] = total(mid, n_b).astype(BF)
+    send_parts(2, n_a, a, at_a, lambda p: fin.at[a], fin)
+    wait_parts(2, n_a, fin)
+    for j in range(n_a):
+        flat[j * chunk : (j + 1) * chunk] = fin[j].astype(F32) * scale
+    unpack(0, g1_ref, gb1_ref)
+    unpack(FLAT, g2_ref, gb2_ref)
 
 
 def write_out(*refs):
@@ -525,10 +472,9 @@
 def solution(mesh):
     n_sy = mesh.shape["sy"]
     n_grp = mesh.shape["grp"]
-    n_m = 2 * n_sy
-    chunk = -(-FLAT // n_m)
+    n_a, n_b = 4 * n_sy, n_grp // 2
+    chunk = -(-2 * FLAT // (2 * n_a)) * 2
     scale = float((n_grp * n_sy * RB * 2 * CB) ** -0.5)
-    most = max(n_m, n_grp)
     shapes = [
         jax.ShapeDtypeStruct((CH, RB, CB), BF),
         jax.ShapeDtypeStruct((CH, RB, CB), BF),
@@ -560,6 +506,7 @@
             pltpu.VMEM((RW + 2, 3 * CH, CW), BF),
             pltpu.VMEM((RW + 6, CH, CW), F32),
             pltpu.VMEM((RW + 4, CH, CW), BF),
+            pltpu.VMEM((RW + 4, CH, CW), BF),
             pltpu.VMEM((2 * CH, 12 * CH), BF),
             pltpu.VMEM((2 * CH, 12 * CH), BF),
             pltpu.VMEM((2 * CH, 12 * CH), BF),
@@ -569,19 +516,15 @@
             pltpu.VMEM((RW, CH, CB), BF),
             pltpu.VMEM((RW, CH, CB), BF),
             pltpu.VMEM((208, 192), F32),
-            pltpu.VMEM((FLAT, 128), F32),
-            pltpu.VMEM((n_m, chunk, 128), F32),
-            pltpu.VMEM((n_m, chunk, 128), F32),
-            pltpu.VMEM((n_m, chunk, 128), F32),
-            pltpu.VMEM((n_m, chunk, 128), F32),
-            pltpu.VMEM((n_grp, chunk, 128), F32),
-            pltpu.VMEM((n_grp, chunk, 128), F32),
-            pltpu.VMEM((n_m, chunk, 128), F32),
-            pltpu.VMEM((n_m, chunk, 128), F32),
+            pltpu.VMEM((n_a * chunk, 128), F32),
+            pltpu.VMEM((n_a, chunk, 128), F32),
+            pltpu.VMEM((n_a, chunk, 128), F32),
+            pltpu.VMEM((n_b, chunk, 128), F32),
+            pltpu.VMEM((n_a, chunk, 128), BF),
             pltpu.SemaphoreType.DMA((4, 4)),
             pltpu.SemaphoreType.DMA((4, 3)),
-            pltpu.SemaphoreType.DMA((6, most)),
-            pltpu.SemaphoreType.DMA((6, most)),
+            pltpu.SemaphoreType.DMA((3,)),
+            pltpu.SemaphoreType.DMA((3,)),
             pltpu.SemaphoreType.DMA((12,)),
         ],
         compiler_params=pltpu.CompilerParams(

time: 42.2 us -> 39.4 us (0.934)
  Pallas kernels: 41.5 us -> 38.6 us
    pallas_call x1, Pallas kernels: 40.3 us -> 37.4 us  [local(): call(*(pltpu.with_memory_space_constraint(v, pltpu.HBM) for v in (image[0...]
where the time goes in v3:
time: 39.4 us; the launch traced here: 39.3 us
  Pallas kernels  38.6 us (98%)
  between operations  0.64 us (2%)
    pallas_call x1, Pallas kernels, local(): call(*(pltpu.with_memory_space_constraint(v, pltpu.HBM) for v in (image[0...  37.4 us
    pallas_call x1, Pallas kernels, local(): store(*call(*(pltpu.with_memory_space_constraint(v, pltpu.HBM) for v in (...  1.22 us

profile of v3, /device:TPU:1, one launch (start us, length us, event | category | flops | bytes accessed | tf_op | source)
XLA Modules:
  0.0 39.3 jit_solution(8429814990303588357)
XLA Ops:
  0.6 37.4 %blocks.1 = (bf16[64,32,128]{2,1,0:T(8,128)(2,1)S(1)}, bf16[64,32,128]{2,1,0:T(8,128)(2,1)S(1)}, f32[3,192,64]{2,1,0:T(8,128)S(1)}, f32[1,64]{1,0:T(1,128)S(1)},...) custom-call(bf16[64,32,128]{2,1,0:T(8,128)(2,1)} %bitcast.10, bf16[64,32,128]{2,1,0:T(8,128)(2,1)} %bitcast.11, ...), custom_call_target="tpu_custom_call" | custom-call | tf_op jit(solution)/shard_map/blocks/pallas_call | solution.py:547
  38.0 1.2 %write_out.1 = (bf16[64,32,128]{2,1,0:T(8,128)(2,1)}, bf16[64,32,128]{2,1,0:T(8,128)(2,1)}, f32[3,192,64]{2,1,0:T(8,128)}, f32[1,64]{1,0:T(1,128)}, f32[3,192,64]{2,1,0:T(8,128)}, /*index=5*/f32[1,64]{1,0:T(1,128)}) custom-call(bf16[64,32,128]{2,1,0:T(8,128)(2,1)S(1)} %get-tuple-element.18.refs_0_, bf16[64,32,128]{2,1,0:T(8,128)(2,1)S(1)} %get-tuple-element.19.refs_1_, ...), custom_call_target="tpu_custom_call" | custom-call | tf_op jit(solution)/shard_map/write_out/pallas_call | solution.py:546

commit v4 on v3

--- a/solution.py
+++ b/solution.py
@@ -107,8 +107,6 @@
     n_y = n_sy // 2
     n_a, n_b = 8 * n_y, n_grp // 2
     z, x_lo = grp // 2, lax.rem(grp, 2)
-    a = ((sy // n_y * 2 + x_lo) * n_y + lax.rem(sy, n_y)) * 2 + sx
-    b = z
     chunk = part.shape[1]
 
     loads = [
@@ -130,17 +128,29 @@
     for load in loads:
         load.start()
 
-    def at_a(p):
-        spot = p // 2
-        x = spot // n_y
-        return {
-            "sy": x // 2 * n_y + lax.rem(spot, n_y),
-            "sx": lax.rem(p, 2),
-            "grp": z * 2 + lax.rem(x, 2),
-        }
-
-    def at_b(p):
-        return {"grp": p * 2 + x_lo}
+    x, y = sy // n_y * 2 + x_lo, lax.rem(sy, n_y)
+    a, b = (x * n_y + y) * 2 + sx, z
+
+    def ring(step, size):
+        return min(step, size - step)
+
+    offsets_a = [
+        (dx, dy, dc) for dx in range(4) for dy in range(n_y) for dc in range(2) if dx + dy + dc
+    ]
+    offsets_a.sort(key=lambda o: -2 * ring(o[0], 4) - 2 * ring(o[1], n_y) - o[2])
+    group_a = []
+    for dx, dy, dc in offsets_a:
+        px, py, pc = lax.rem(x + dx, 4), lax.rem(y + dy, n_y), lax.rem(sx + dc, 2)
+        group_a.append(
+            (
+                (px * n_y + py) * 2 + pc,
+                {"sy": px // 2 * n_y + py, "sx": pc, "grp": z * 2 + lax.rem(px, 2)},
+            )
+        )
+    group_b = []
+    for dz in sorted(range(1, n_b), key=lambda o: -ring(o, n_b)):
+        pz = lax.rem(z + dz, n_b)
+        group_b.append((pz, {"grp": pz * 2 + x_lo}))
 
     has_down = sy < n_sy - 1
     has_up = sy > 0
@@ -148,14 +158,8 @@
 
     barrier = pltpu.get_barrier_semaphore()
 
-    for d in range(1, n_b):
-        pl.semaphore_signal(
-            barrier, inc=1, device_id=at_b(lax.rem(b + d, n_b)), device_id_type=MESH
-        )
-    for d in range(1, n_a):
-        pl.semaphore_signal(
-            barrier, inc=1, device_id=at_a(lax.rem(a + d, n_a)), device_id_type=MESH
-        )
+    for _, where in group_a + group_b:
+        pl.semaphore_signal(barrier, inc=1, device_id=where, device_id_type=MESH)
 
     lane = lax.broadcasted_iota(jnp.int32, (CH, CW), 1)
     mine = pl.multiple_of(sx * CB, CB)
@@ -375,15 +379,14 @@
         flat[base + 192 : base + 288] = jnp.concatenate([tail[0:96], tail[96:192]], 1)
         flat[base + 288 : base + FLAT] = gacc[192:200, 0:128]
 
-    def send_parts(i, count, me, where, source, landing):
-        for d in range(1, count):
-            p = lax.rem(me + d, count)
+    def send_parts(i, group, me, source, landing):
+        for p, where in group:
             pltpu.make_async_remote_copy(
                 src_ref=source(p),
                 dst_ref=landing.at[me],
                 send_sem=send_red.at[i],
                 recv_sem=recv_red.at[i],
-                device_id=where(p),
+                device_id=where,
                 device_id_type=MESH,
             ).start()
 
@@ -432,7 +435,7 @@
     kernel_grad(h3, 2, dz2, FLAT)
     for j in range(n_a):
         part[j] = flat[j * chunk : (j + 1) * chunk]
-    send_parts(0, n_a, a, at_a, lambda p: part.at[p], landed)
+    send_parts(0, group_a, a, lambda p: part.at[p], landed)
     landed[a] = part[a]
     pair_copy(0, outw.at[pl.ds(2, RW)], outs).start()
 
@@ -445,12 +448,12 @@
 
     wait_parts(0, n_a, landed)
     mid[b] = total(landed, n_a)
-    send_parts(1, n_b, b, at_b, lambda p: mid.at[b], mid)
+    send_parts(1, group_b, b, lambda p: mid.at[b], mid)
     channels_major(1, igw, igs, ig_ref)
 
     wait_parts(1, n_b, mid)
     fin[a] = total(mid, n_b).astype(BF)
-    send_parts(2, n_a, a, at_a, lambda p: fin.at[a], fin)
+    send_parts(2, group_a, a, lambda p: fin.at[a], fin)
     wait_parts(2, n_a, fin)
     for j in range(n_a):
         flat[j * chunk : (j + 1) * chunk] = fin[j].astype(F32) * scale

time: 39.4 us -> 36.9 us (0.937)
  Pallas kernels: 38.6 us -> 36.2 us
    pallas_call x1, Pallas kernels: 37.4 us -> 35 us  [local(): call(*(pltpu.with_memory_space_constraint(v, pltpu.HBM) for v in (image[0...]
where the time goes in v4:
time: 36.9 us; the launch traced here: 36.8 us
  Pallas kernels  36.2 us (98%)
  between operations  0.64 us (2%)
    pallas_call x1, Pallas kernels, local(): call(*(pltpu.with_memory_space_constraint(v, pltpu.HBM) for v in (image[0...  35 us
    pallas_call x1, Pallas kernels, local(): store(*call(*(pltpu.with_memory_space_constraint(v, pltpu.HBM) for v in (...  1.22 us

profile of v4, /device:TPU:1, one launch (start us, length us, event | category | flops | bytes accessed | tf_op | source)
XLA Modules:
  0.0 36.8 jit_solution(12689814386715030)
XLA Ops:
  0.6 35.0 %blocks.1 = (bf16[64,32,128]{2,1,0:T(8,128)(2,1)S(1)}, bf16[64,32,128]{2,1,0:T(8,128)(2,1)S(1)}, f32[3,192,64]{2,1,0:T(8,128)S(1)}, f32[1,64]{1,0:T(1,128)S(1)},...) custom-call(bf16[64,32,128]{2,1,0:T(8,128)(2,1)} %bitcast.10, bf16[64,32,128]{2,1,0:T(8,128)(2,1)} %bitcast.11, ...), custom_call_target="tpu_custom_call" | custom-call | tf_op jit(solution)/shard_map/blocks/pallas_call | solution.py:550
  35.6 1.2 %write_out.1 = (bf16[64,32,128]{2,1,0:T(8,128)(2,1)}, bf16[64,32,128]{2,1,0:T(8,128)(2,1)}, f32[3,192,64]{2,1,0:T(8,128)}, f32[1,64]{1,0:T(1,128)}, f32[3,192,64]{2,1,0:T(8,128)}, /*index=5*/f32[1,64]{1,0:T(1,128)}) custom-call(bf16[64,32,128]{2,1,0:T(8,128)(2,1)S(1)} %get-tuple-element.18.refs_0_, bf16[64,32,128]{2,1,0:T(8,128)(2,1)S(1)} %get-tuple-element.19.refs_1_, ...), custom_call_target="tpu_custom_call" | custom-call | tf_op jit(solution)/shard_map/write_out/pallas_call | solution.py:549

commit v5 on v4

--- a/solution.py
+++ b/solution.py
@@ -100,6 +100,7 @@
     send_red,
     recv_red,
     load_sem,
+    entered,
 ):
     sy = lax.axis_index("sy")
     sx = lax.axis_index("sx")
@@ -139,6 +140,7 @@
     ]
     offsets_a.sort(key=lambda o: -2 * ring(o[0], 4) - 2 * ring(o[1], n_y) - o[2])
     group_a = []
+    close = []
     for dx, dy, dc in offsets_a:
         px, py, pc = lax.rem(x + dx, 4), lax.rem(y + dy, n_y), lax.rem(sx + dc, 2)
         group_a.append(
@@ -147,10 +149,14 @@
                 {"sy": px // 2 * n_y + py, "sx": pc, "grp": z * 2 + lax.rem(px, 2)},
             )
         )
+        if ring(dx, 4) + ring(dy, n_y) <= 1:
+            close.append(group_a[-1][1])
     group_b = []
     for dz in sorted(range(1, n_b), key=lambda o: -ring(o, n_b)):
         pz = lax.rem(z + dz, n_b)
         group_b.append((pz, {"grp": pz * 2 + x_lo}))
+        if ring(dz, n_b) <= 1:
+            close.append(group_b[-1][1])
 
     has_down = sy < n_sy - 1
     has_up = sy > 0
@@ -158,8 +164,18 @@
 
     barrier = pltpu.get_barrier_semaphore()
 
-    for _, where in group_a + group_b:
+    for where in close:
         pl.semaphore_signal(barrier, inc=1, device_id=where, device_id_type=MESH)
+
+    @pl.when(takes)
+    def _():
+        for core in range(2):
+            pl.semaphore_signal(
+                barrier,
+                inc=1,
+                device_id={"sy": sy - 1 + 2 * sx, "sx": core},
+                device_id_type=MESH,
+            )
 
     lane = lax.broadcasted_iota(jnp.int32, (CH, CW), 1)
     mine = pl.multiple_of(sx * CB, CB)
@@ -252,8 +268,19 @@
                 ).wait_recv()
 
     rows_major(0, x_ref, xt)
-    pl.semaphore_wait(barrier, n_a - 1 + n_b - 1)
+    pl.semaphore_wait(
+        barrier, len(close) + has_down.astype(jnp.int32) + has_up.astype(jnp.int32)
+    )
+
+    def tell(i):
+        for where in close:
+            pl.semaphore_signal(entered.at[i], inc=1, device_id=where, device_id_type=MESH)
+
+    def hear(i):
+        pl.semaphore_wait(entered.at[i], len(close))
+
     halo_start(0, xt, xw, 4)
+    tell(0)
     rows_major(4, ct_ref, ctt)
     halo_start(1, ctt, ctw, 2)
 
@@ -315,9 +342,14 @@
     halo_wait_pair(0, xt, xw, 4)
     each(RW + 4, lambda r: store_shifted(xw[r + 4 - 4 * sx], x3, r + 4 - 4 * sx, lane))
     each(RW // 2 + 1, lambda k: hidden_rows(k + 2 - 2 * sx))
+    hear(0)
+    tell(1)
     halo_wait_pair(1, ctt, ctw, 2)
     each(RW // 2, lambda k: output_rows(k + 2 - 2 * sx))
     each(RW // 2 - 1, lambda k: delta_rows(k + 2 - 2 * sx))
+
+    hear(1)
+    tell(2)
 
     halo_wait_far(0, xt, xw, 4)
     each(4, lambda r: store_shifted(xw[r + (RW + 4) * sx], x3, r + (RW + 4) * sx, lane))
@@ -435,6 +467,7 @@
     kernel_grad(h3, 2, dz2, FLAT)
     for j in range(n_a):
         part[j] = flat[j * chunk : (j + 1) * chunk]
+    hear(2)
     send_parts(0, group_a, a, lambda p: part.at[p], landed)
     landed[a] = part[a]
     pair_copy(0, outw.at[pl.ds(2, RW)], outs).start()
@@ -529,6 +562,7 @@
             pltpu.SemaphoreType.DMA((3,)),
             pltpu.SemaphoreType.DMA((3,)),
             pltpu.SemaphoreType.DMA((12,)),
+            pltpu.SemaphoreType.REGULAR((3,)),
         ],
         compiler_params=pltpu.CompilerParams(
             collective_id=0, has_side_effects=True, vmem_limit_bytes=50 * 1024 * 1024

time: 36.9 us -> 35.8 us (0.970)
  Pallas kernels: 36.2 us -> 35 us
    pallas_call x1, Pallas kernels: 35 us -> 33.8 us  [local(): call(*(pltpu.with_memory_space_constraint(v, pltpu.HBM) for v in (image[0...]
where the time goes in v5:
time: 35.8 us; the launch traced here: 35.7 us
  Pallas kernels  35 us (98%)
  between operations  0.64 us (2%)
    pallas_call x1, Pallas kernels, local(): call(*(pltpu.with_memory_space_constraint(v, pltpu.HBM) for v in (image[0...  33.8 us
    pallas_call x1, Pallas kernels, local(): store(*call(*(pltpu.with_memory_space_constraint(v, pltpu.HBM) for v in (...  1.22 us

profile of v5, /device:TPU:1, one launch (start us, length us, event | category | flops | bytes accessed | tf_op | source)
XLA Modules:
  0.0 35.7 jit_solution(13507361006074203156)
XLA Ops:
  0.6 33.8 %blocks.1 = (bf16[64,32,128]{2,1,0:T(8,128)(2,1)S(1)}, bf16[64,32,128]{2,1,0:T(8,128)(2,1)S(1)}, f32[3,192,64]{2,1,0:T(8,128)S(1)}, f32[1,64]{1,0:T(1,128)S(1)},...) custom-call(bf16[64,32,128]{2,1,0:T(8,128)(2,1)} %bitcast.10, bf16[64,32,128]{2,1,0:T(8,128)(2,1)} %bitcast.11, ...), custom_call_target="tpu_custom_call" | custom-call | tf_op jit(solution)/shard_map/blocks/pallas_call | solution.py:584
  34.4 1.2 %write_out.1 = (bf16[64,32,128]{2,1,0:T(8,128)(2,1)}, bf16[64,32,128]{2,1,0:T(8,128)(2,1)}, f32[3,192,64]{2,1,0:T(8,128)}, f32[1,64]{1,0:T(1,128)}, f32[3,192,64]{2,1,0:T(8,128)}, /*index=5*/f32[1,64]{1,0:T(1,128)}) custom-call(bf16[64,32,128]{2,1,0:T(8,128)(2,1)S(1)} %get-tuple-element.18.refs_0_, bf16[64,32,128]{2,1,0:T(8,128)(2,1)S(1)} %get-tuple-element.19.refs_1_, ...), custom_call_target="tpu_custom_call" | custom-call | tf_op jit(solution)/shard_map/write_out/pallas_call | solution.py:583
